TPU v7x, 32 devices: a whole 2x2x4 slice. The times are simulated.
32 devices in a mesh: lon: 16 (over z, y, core), lat: 2 (over x).
Axes of the slice: x: 2, y: 2, z: 4, core: 2. Of those that a mesh axis runs over, the one named last changes fastest.
Arguments:
- field: bfloat16 [1, 64, 256, 256], P(None, 'lat', 'lon'), may hold values from -6 to 6
- depth_kernel: float32 [7, 7, 256], replicated, may hold values from -0.875 to 0.875
- layer_norm_gain: float32 [256], replicated, may hold values from 0.1 to 1.9
- inner_weight: bfloat16 [256, 1024], replicated, may hold values from -0.375 to 0.375
- outer_weight: bfloat16 [1024, 256], replicated, may hold values from -0.1875 to 0.1875
- layer_scale: float32 [256], replicated, may hold values from 0.3 to 1.5
- down_weight: bfloat16 [1024, 512], replicated, may hold values from -0.1875 to 0.1875
- cotangent: bfloat16 [1, 32, 128, 512], P(None, 'lat', 'lon'), may hold values from -6 to 6
Outputs:
- coarse: bfloat16 [1, 32, 128, 512], P(None, 'lat', 'lon')
- grad_field: bfloat16 [1, 64, 256, 256], P(None, 'lat', 'lon')
- grad_kernel: float32 [7, 7, 256], replicated
- grad_gain: float32 [256], replicated
- grad_inner: float32 [256, 1024], replicated
- grad_outer: float32 [1024, 256], replicated
- grad_scale: float32 [256], replicated
- grad_down: float32 [1024, 512], replicated
All inputs are finite; a program needn't handle non-finite values.
Results may differ from a plain program's by a relative error of at most 0.0071.
Values may be sent and summed in bfloat16 or wider, within the bound.
A program may use at most 64 MiB of HBM per device.

v0:
```python
from functools import partial
import math

import jax
import jax.numpy as jnp
from jax import lax
from jax.sharding import PartitionSpec as P

PARAMS = 1061632


EPS = 1e-06


def padded_2(cells, sides, width, closed):
    for axis, dim in sides:
        count = lax.axis_size(axis)
        ends = count if closed else count - 1
        head = lax.slice_in_dim(cells, 0, width, axis=dim)
        tail = lax.slice_in_dim(cells, cells.shape[dim] - width, cells.shape[dim], axis=dim)
        cells = jnp.concatenate(
            [
                lax.ppermute(tail, axis, [(i, (i + 1) % count) for i in range(ends)]),
                cells,
                lax.ppermute(head, axis, [((i + 1) % count, i) for i in range(ends)]),
            ],
            axis=dim,
        )
    return cells


def depth_apply(padded, kernel):
    rows = padded.shape[1] - 6
    cols = padded.shape[2] - 6
    total = jnp.zeros((padded.shape[0], rows, cols, padded.shape[3]), jnp.float32)
    for row_shift in range(7):
        for col_shift in range(7):
            total = (
                total
                + kernel[row_shift, col_shift]
                * padded[:, row_shift : row_shift + rows, col_shift : col_shift + cols]
            )
    return total


def depth_transpose(padded, kernel):
    rows = padded.shape[1] - 6
    cols = padded.shape[2] - 6
    total = jnp.zeros((padded.shape[0], rows, cols, padded.shape[3]), jnp.float32)
    for row_shift in range(7):
        for col_shift in range(7):
            total = (
                total
                + kernel[row_shift, col_shift]
                * padded[
                    :, 6 - row_shift : 6 - row_shift + rows, 6 - col_shift : 6 - col_shift + cols
                ]
            )
    return total


def kernel_terms(padded, grad):
    rows = grad.shape[1]
    cols = grad.shape[2]
    terms = []
    for row_shift in range(7):
        for col_shift in range(7):
            terms.append(
                jnp.sum(
                    padded[:, row_shift : row_shift + rows, col_shift : col_shift + cols] * grad,
                    axis=(0, 1, 2),
                )
            )
    return jnp.stack(terms).reshape(7, 7, grad.shape[3])


def to_patches(values):
    batch, rows, cols, channel_count = values.shape
    return (
        values.reshape(batch, rows // 2, 2, cols // 2, 2, channel_count)
        .transpose(0, 1, 3, 2, 4, 5)
        .reshape(-1, 4 * channel_count)
    )


def from_patches(values, shape):
    batch, rows, cols, channel_count = shape
    return (
        values.reshape(batch, rows // 2, cols // 2, 2, 2, channel_count)
        .transpose(0, 1, 3, 2, 4, 5)
        .reshape(batch, rows, cols, channel_count)
    )


def reduce_down(raw_down):
    return lax.psum(raw_down, ("lon", "lat"))


def body(
    field,
    depth_kernel,
    layer_norm_gain,
    inner_weight,
    outer_weight,
    layer_scale,
    down_weight,
    cotangent,
):
    channel_count = field.shape[3]
    wide = padded_2(field, (("lon", 2),), 3, True)
    padded = padded_2(wide, (("lat", 1),), 3, False)
    mixed = depth_apply(padded.astype(jnp.float32), depth_kernel)
    centered_input = mixed - jnp.mean(mixed, axis=-1, keepdims=True)
    inverse_deviation = lax.rsqrt(
        jnp.mean(centered_input * centered_input, axis=-1, keepdims=True) + EPS
    )
    standardized_input = centered_input * inverse_deviation
    normalized_output = (
        (standardized_input * layer_norm_gain).astype(jnp.bfloat16).reshape(-1, channel_count)
    )
    preact = jnp.dot(normalized_output, inner_weight, preferred_element_type=jnp.float32)
    hidden = jax.nn.gelu(preact, approximate=False).astype(jnp.bfloat16)
    branch = jnp.dot(hidden, outer_weight, preferred_element_type=jnp.float32)
    blocked = (field.astype(jnp.float32).reshape(-1, channel_count) + layer_scale * branch).astype(
        jnp.bfloat16
    )
    patches = to_patches(blocked.reshape(field.shape))
    coarse = jnp.dot(patches, down_weight, preferred_element_type=jnp.float32).astype(jnp.bfloat16)
    coarse = coarse.reshape(cotangent.shape)
    flat_grad = cotangent.reshape(-1, cotangent.shape[3])
    raw_down = jnp.dot(patches.T, flat_grad, preferred_element_type=jnp.float32)
    grad_patch = jnp.dot(flat_grad, down_weight.T, preferred_element_type=jnp.float32).astype(
        jnp.bfloat16
    )
    grad_blocked = from_patches(grad_patch, field.shape).reshape(-1, channel_count)
    raw_scale = jnp.sum(grad_blocked.astype(jnp.float32) * branch, axis=0)
    grad_branch = (grad_blocked.astype(jnp.float32) * layer_scale).astype(jnp.bfloat16)
    grad_hidden = jnp.dot(grad_branch, outer_weight.T, preferred_element_type=jnp.float32)
    grad_pre = jax.vjp(partial(jax.nn.gelu, approximate=False), preact)[1](grad_hidden)[0].astype(
        jnp.bfloat16
    )
    raw_outer = jnp.dot(hidden.T, grad_branch, preferred_element_type=jnp.float32)
    raw_inner = jnp.dot(normalized_output.T, grad_pre, preferred_element_type=jnp.float32)
    normalized_gradient = jnp.dot(
        grad_pre, inner_weight.T, preferred_element_type=jnp.float32
    ).reshape(mixed.shape)
    unclipped_gain = jnp.sum(normalized_gradient * standardized_input, axis=(0, 1, 2))
    gain_scaled_output = normalized_gradient * layer_norm_gain
    depthwise_gradient = (
        gain_scaled_output
        - jnp.mean(gain_scaled_output, axis=-1, keepdims=True)
        - standardized_input
        * jnp.mean(gain_scaled_output * standardized_input, axis=-1, keepdims=True)
    ) * inverse_deviation
    depthwise_gradient = depthwise_gradient.astype(jnp.bfloat16)
    grad_wide = padded_2(depthwise_gradient, (("lon", 2),), 3, True)
    grad_padded = padded_2(grad_wide, (("lat", 1),), 3, False).astype(jnp.float32)
    spread = depth_transpose(grad_padded, depth_kernel)
    grad_field = (grad_blocked.reshape(field.shape).astype(jnp.float32) + spread).astype(
        jnp.bfloat16
    )
    raw_kernel = kernel_terms(padded.astype(jnp.float32), depthwise_gradient.astype(jnp.float32))
    summed_down = reduce_down(raw_down)
    limit = math.sqrt(PARAMS)
    sum_kernel, sum_gain, sum_inner, sum_outer, sum_scale = lax.psum(
        (raw_kernel, unclipped_gain, raw_inner, raw_outer, raw_scale), ("lon", "lat")
    )
    total = (
        jnp.sum(sum_kernel * sum_kernel)
        + jnp.sum(sum_gain * sum_gain)
        + jnp.sum(sum_inner * sum_inner)
        + jnp.sum(sum_outer * sum_outer)
        + jnp.sum(sum_scale * sum_scale)
        + jnp.sum(summed_down * summed_down)
    )
    factor = jnp.minimum(1.0, limit / jnp.sqrt(total + EPS))
    grad_kernel = sum_kernel * factor
    grad_gain = sum_gain * factor
    grad_inner = sum_inner * factor
    grad_outer = sum_outer * factor
    grad_scale = sum_scale * factor
    grad_down = summed_down * factor
    return (
        coarse,
        grad_field,
        grad_kernel,
        grad_gain,
        grad_inner,
        grad_outer,
        grad_scale,
        grad_down,
    )


def solution(mesh):
    return jax.shard_map(
        body,
        mesh=mesh,
        in_specs=(
            P(None, "lat", "lon", None),
            P(),
            P(),
            P(),
            P(),
            P(),
            P(),
            P(None, "lat", "lon", None),
        ),
        out_specs=(
            P(None, "lat", "lon", None),
            P(None, "lat", "lon", None),
            P(),
            P(),
            P(),
            P(),
            P(),
            P(),
        ),
        check_vma=False,
    )
```

profile of v0, /device:TPU:0, one launch (start us, length us, event | category | flops | bytes accessed | tf_op | source)
XLA Modules:
  0.0 220.6 jit_solution(751683770909935926)
XLA Ops:
  7.2 1.1 fusion.114
  8.8 5.1 %collective-permute-start.1 = (bf16[1,32,3,256]{3,2,1,0:T(4,128)(2,1)S(1)}, bf16[1,32,3,256]{3,2,1,0:T(4,128)(2,1)S(1)}, u32[]{:S(2)}, u32[]{:S(2)}) collective-permute-start(bf16[1,32,3,256]{3,2,1,0:T(4,128)(2,1)S(1)} %get-tuple-element.79), channel_id=1, source_target_pairs={{2,0},{4,2},{6,4},{8,6},{10,8},{12,10},{14,12},{16,14},{18,16},{20... | collective-permute-start | bytes 147464 | tf_op jit(solution)/shard_map/ppermute | solution.py:25
  13.9 1.0 fusion.115
  15.1 1.4 convolution_convert_fusion
  16.5 1.0 fusion.116
  17.8 0.8 pad_maximum_fusion.5
  18.6 3.8 %collective-permute-start.2 = (bf16[1,3,22,256]{3,2,1,0:T(8,128)(2,1)S(1)}, bf16[1,3,22,256]{3,2,1,0:T(8,128)(2,1)S(1)}, u32[]{:S(2)}, u32[]{:S(2)}) collective-permute-start(bf16[1,3,22,256]{3,2,1,0:T(8,128)(2,1)S(1)} %get-tuple-element.74), channel_id=1, source_target_pairs={{0,1},{2,3},{4,5},{6,7},{8,9},{10,11},{12,13},{14,15},{16,17},{18,... | collective-permute-start | bytes 101384 | tf_op jit(solution)/shard_map/ppermute | solution.py:23
  22.4 1.3 collective-permute-start.3
  23.7 1.5 fusion.117
  25.8 1.2 reshape.366
  26.9 1.3 collective-permute-done.3
  28.8 4.5 %fusion.112 = (f32[32,16]{1,0:T(8,128)S(1)}, f32[1,32,16,256]{3,2,1,0:T(8,128)S(1)}) fusion(f32[1,38,22,256]{3,2,1,0:T(8,128)S(1)} %maximum_convert_fusion, f32[256]{0:T(256)} %bitcast.49, f32[256]{0:T(256)} %bitcast.48, f32[256]{0:T(256)S(1)} %bitcast.144, f32[256]{0:T(256)S(1)} %bitcast.146, f32[256]{0:T(256)S(1)} %bitcast.148, f32[256]{0:T(256)S(1)} %bitcast.150, ...), kind=kLoop, calls=%fused_computation.259 | loop fusion | flops 12844544 | bytes 26266624 | tf_op jit(solution)/shard_map/reduce_sum | solution.py:113
  34.3 5.8 %multiply_convert_fusion = (bf16[512,1024]{1,0:T(8,128)(2,1)S(1)}, f32[512,1024]{1,0:T(8,128)S(1)}, f32[512,1024]{1,0:T(8,128)S(1)}) fusion(bf16[512,256]{1,0:T(8,128)(2,1)S(1)} %bitcast.138, bf16[256,1024]{1,0:T(8,128)(2,1)S(1)} %copy-done.98), kind=kOutput, calls=%fused_computation.53 | convolution fusion | flops 302514176 | bytes 6029312 | tf_op jit(solution)/shard_map/dot_general | solution.py:121
  40.1 1.5 fusion.110
  41.6 1.0 multiply_reduce_fusion.3
  42.6 1.0 add_convert_fusion
  43.6 1.1 multiply_reduce_fusion.6
  44.8 1.4 fusion.118
  46.3 0.9 copy.22
  47.2 1.1 reshape.359
  48.4 0.7 broadcast_multiply_fusion.6
  49.0 0.7 div.20
  49.7 1.6 multiply_reduce_fusion.4
  51.3 3.0 %fusion.54 = (f32[256]{0:T(256)}, f32[256]{0:T(256)}, f32[256]{0:T(256)}, f32[256]{0:T(256)}, f32[256]{0:T(256)}, /*index=5*/f32[256]{0:T(256)}, f32[256]{0:T(25...) fusion(f32[1,38,22,256]{3,2,1,0:T(8,128)S(1)} %maximum_convert_, ...), kind=kLoop, calls=%fused_computation.120 | loop fusion | flops 5893632 | bytes 10775552 | tf_op jit(solution)/shard_map/reduce_sum | solution.py:69
  54.3 1.1 fusion.55
  55.4 1.8 fusion.107
  57.2 0.7 fusion.53
  58.3 2.9 %stack.199 = f32[49,256]{1,0:T(8,128)S(1)} concatenate(f32[1,256]{1,0:T(1,128)S(1)} %bitcast.250, f32[1,256]{1,0:T(1,128)S(1)} %bitcast.252, f32[1,256]{1,0:T(1,128)S(1)} %bitcast.253, f32[1,256]{1,0:T(1,128)S(1)} %bitcast.254, f32[1,256]{1,0:T(1,128)S(1)} %bitcast.255, f32[1,256]{1,0:T(1,128)S(1)} %bitcast.256, f32[1,256]{1,0:T(1,128)S(1)} %bitcast.257, f32[1,256]{1,0:T(1,128)S(1)} %bitcast.258, ...), dimensions={0} | concatenate | bytes 100352 | tf_op jit(solution)/shard_map/stack | solution.py:74
  61.4 4.4 %collective-permute-start.5 = (bf16[1,32,3,256]{3,2,1,0:T(4,128)(2,1)S(1)}, bf16[1,32,3,256]{3,2,1,0:T(4,128)(2,1)S(1)}, u32[]{:S(2)}, u32[]{:S(2)}) collective-permute-start(bf16[1,32,3,256]{3,2,1,0:T(4,128)(2,1)S(1)} %get-tuple-element.77), channel_id=1, source_target_pairs={{2,0},{4,2},{6,4},{8,6},{10,8},{12,10},{14,12},{16,14},{18,16},{20... | collective-permute-start | bytes 147464 | tf_op jit(solution)/shard_map/ppermute | solution.py:25
  65.8 38.1 %all-reduce = (f32[7,7,256]{2,1,0:T(8,128)S(1)}, f32[256]{0:T(256)S(1)}, f32[256]{0:T(256)S(1)}) all-reduce(f32[7,7,256]{2,1,0:T(8,128)S(1)} %reshape.363, f32[256]{0:T(256)} %get-tuple-element.57, f32[256]{0:T(256)} %get-tuple-element.70), channel_id=1, replica_groups=mesh['lon'=16,'lat'=2] {'lon','lat'}, use_global_device_ids=true, to_apply=%region_53.0 | all-reduce | flops 13056 | bytes 104448 | tf_op jit(solution)/shard_map/psum | solution.py:165
  104.0 1.0 fusion.6
  105.0 0.6 multiply_reduce_fusion.8
  105.6 4.2 %collective-permute-start.6 = (bf16[1,3,22,256]{3,2,1,0:T(8,128)(2,1)S(1)}, bf16[1,3,22,256]{3,2,1,0:T(8,128)(2,1)S(1)}, u32[]{:S(2)}, u32[]{:S(2)}) collective-permute-start(bf16[1,3,22,256]{3,2,1,0:T(8,128)(2,1)S(1)} %get-tuple-element.72), channel_id=1, source_target_pairs={{0,1},{2,3},{4,5},{6,7},{8,9},{10,11},{12,13},{14,15},{16,17},{18,... | collective-permute-start | bytes 101384 | tf_op jit(solution)/shard_map/ppermute | solution.py:23
  109.8 1.3 collective-permute-start.7
  111.1 0.7 multiply_reduce_fusion.9
  113.0 2.6 %collective-permute-done.7 = bf16[1,3,22,256]{3,2,1,0:T(8,128)(2,1)S(1)} collective-permute-done((bf16[1,3,22,256]{3,2,1,0:T(8,128)(2,1)S(1)}, bf16[1,3,22,256]{3,2,1,0:T(8,128)(2,1)S(1)}, u32[]{:S(2)}, u32[]{:S(2)}) %collective-permute-start.7) | collective-permute-done | bytes 33824 | tf_op jit(solution)/shard_map/ppermute | solution.py:25
  116.2 5.1 %fusion.58 = bf16[1,32,16,256]{3,2,1,0:T(8,128)(2,1)} fusion(f32[1,32,16,256]{3,2,1,0:T(8,128)S(1)} %copy-done.7, f32[1,38,22,256]{3,2,1,0:T(8,128)S(1)} %maximum_convert_fusion.1, f32[256]{0:T(256)} %bitcast.49, f32[256]{0:T(256)} %bitcast.48, f32[256]{0:T(256)S(1)} %bitcast.145, f32[256]{0:T(256)S(1)} %bitcast.147, f32[256]{0:T(256)S(1)} %bitcast.149, ...), kind=kLoop, calls=%fused_computation.125 | loop fusion | flops 12976128 | bytes 26526720 | tf_op jit(solution)/shard_map/convert_element_type | solution.py:159
  121.3 79.2 %all-reduce.4.cloned.1.call-done = (f32[256,1024]{1,0:T(8,128)}, f32[1024,256]{1,0:T(8,128)}, f32[1024,512]{1,0:T(8,128)}) async-done(((f32[256,1024]{1,0:T(8,128)}, f32[1024,256]{1,0:T(8,128)}, f32[1024,512]{1,0:T(8,128)}), (f32[256,1024]{1,0:T(8,128)}, f32[1024,256]{1,0:T(8,128)}, f32[1024,512]{1,0:T(8,128)})) %all-reduce.4.cloned.1.call-update) | async-done | bytes 4194320 | tf_op jit(solution)/shard_map/psum | solution.py:165
  200.5 2.9 %multiply_reduce_fusion = f32[]{:T(128)} fusion(f32[1024,512]{1,0:T(8,128)} %get-tuple-element.64), kind=kLoop, calls=%fused_computation.51 | loop fusion | flops 1048575 | bytes 2097156 | tf_op jit(solution)/shard_map/reduce_sum | solution.py:174
  203.3 0.9 multiply_reduce_fusion.1
  204.2 0.9 multiply_reduce_fusion.2
  207.8 0.6 broadcast_multiply_fusion.7
  208.3 1.5 broadcast_multiply_fusion
  209.9 1.0 broadcast_multiply_fusion.1
  210.9 0.6 copy-done.3
  211.5 1.1 broadcast_multiply_fusion.2
  212.6 0.6 broadcast_multiply_fusion.8
  213.1 0.6 broadcast_multiply_fusion.3
  (220 shorter events, 3.0 us)
Async XLA Ops:
  7.2 193.3 %all-reduce.4.cloned.1.call-start = ((), (), s32[]{:S(2)}) async-start(), calls=%async_computation | async-start | bytes 8388608 | tf_op jit(solution)/shard_map/psum | solution.py:165
  8.3 9.4 %collective-permute-start = (bf16[1,32,3,256]{3,2,1,0:T(4,128)(2,1)S(1)}, bf16[1,32,3,256]{3,2,1,0:T(4,128)(2,1)S(1)}, u32[]{:S(2)}, u32[]{:S(2)}) collective-permute-start(bf16[1,32,3,256]{3,2,1,0:T(4,128)(2,1)S(1)} %get-tuple-element.78), channel_id=1, source_target_pairs={{0,2},{2,4},{4,6},{6,8},{8,10},{10,12},{12,14},{14,16},{16,18},{18... | collective-permute-start | bytes 147464 | tf_op jit(solution)/shard_map/ppermute | solution.py:23
  8.8 8.9 %collective-permute-start.1 = (bf16[1,32,3,256]{3,2,1,0:T(4,128)(2,1)S(1)}, bf16[1,32,3,256]{3,2,1,0:T(4,128)(2,1)S(1)}, u32[]{:S(2)}, u32[]{:S(2)}) collective-permute-start(bf16[1,32,3,256]{3,2,1,0:T(4,128)(2,1)S(1)} %get-tuple-element.79), channel_id=1, source_target_pairs={{2,0},{4,2},{6,4},{8,6},{10,8},{12,10},{14,12},{16,14},{18,16},{20... | collective-permute-start | bytes 147464 | tf_op jit(solution)/shard_map/ppermute | solution.py:25
  18.6 8.4 %collective-permute-start.2 = (bf16[1,3,22,256]{3,2,1,0:T(8,128)(2,1)S(1)}, bf16[1,3,22,256]{3,2,1,0:T(8,128)(2,1)S(1)}, u32[]{:S(2)}, u32[]{:S(2)}) collective-permute-start(bf16[1,3,22,256]{3,2,1,0:T(8,128)(2,1)S(1)} %get-tuple-element.74), channel_id=1, source_target_pairs={{0,1},{2,3},{4,5},{6,7},{8,9},{10,11},{12,13},{14,15},{16,17},{18,... | collective-permute-start | bytes 101384 | tf_op jit(solution)/shard_map/ppermute | solution.py:23
  22.4 5.9 %collective-permute-start.3 = (bf16[1,3,22,256]{3,2,1,0:T(8,128)(2,1)S(1)}, bf16[1,3,22,256]{3,2,1,0:T(8,128)(2,1)S(1)}, u32[]{:S(2)}, u32[]{:S(2)}) collective-permute-start(bf16[1,3,22,256]{3,2,1,0:T(8,128)(2,1)S(1)} %get-tuple-element.75), channel_id=1, source_target_pairs={{1,0},{3,2},{5,4},{7,6},{9,8},{11,10},{13,12},{15,14},{17,16},{19,... | collective-permute-start | bytes 101384 | tf_op jit(solution)/shard_map/ppermute | solution.py:25
  57.9 57.9 %copy-start.16 = (f32[1,1,256]{2,1,0:T(1,128)S(1)}, f32[1,1,256]{2,1,0:T(1,128)}, u32[]{:S(2)}) copy-start(f32[1,1,256]{2,1,0:T(1,128)} %copy-done.15) | copy-start | bytes 3076
  57.9 57.9 %copy-start.18 = (f32[1,1,256]{2,1,0:T(1,128)S(1)}, f32[1,1,256]{2,1,0:T(1,128)}, u32[]{:S(2)}) copy-start(f32[1,1,256]{2,1,0:T(1,128)} %copy-done.17) | copy-start | bytes 3076
  57.9 57.9 %copy-start.20 = (f32[1,1,256]{2,1,0:T(1,128)S(1)}, f32[1,1,256]{2,1,0:T(1,128)}, u32[]{:S(2)}) copy-start(f32[1,1,256]{2,1,0:T(1,128)} %copy-done.19) | copy-start | bytes 3076
  58.0 57.9 %copy-start.22 = (f32[1,1,256]{2,1,0:T(1,128)S(1)}, f32[1,1,256]{2,1,0:T(1,128)}, u32[]{:S(2)}) copy-start(f32[1,1,256]{2,1,0:T(1,128)} %copy-done.21) | copy-start | bytes 3076
  58.0 57.9 %copy-start.24 = (f32[1,1,256]{2,1,0:T(1,128)S(1)}, f32[1,1,256]{2,1,0:T(1,128)}, u32[]{:S(2)}) copy-start(f32[1,1,256]{2,1,0:T(1,128)} %copy-done.23) | copy-start | bytes 3076
  58.0 57.9 %copy-start.26 = (f32[1,1,256]{2,1,0:T(1,128)S(1)}, f32[1,1,256]{2,1,0:T(1,128)}, u32[]{:S(2)}) copy-start(f32[1,1,256]{2,1,0:T(1,128)} %copy-done.25) | copy-start | bytes 3076
  58.0 57.9 %copy-start.28 = (f32[1,1,256]{2,1,0:T(1,128)S(1)}, f32[1,1,256]{2,1,0:T(1,128)}, u32[]{:S(2)}) copy-start(f32[1,1,256]{2,1,0:T(1,128)} %copy-done.27) | copy-start | bytes 3076
  58.0 57.9 %copy-start.30 = (f32[1,1,256]{2,1,0:T(1,128)S(1)}, f32[1,1,256]{2,1,0:T(1,128)}, u32[]{:S(2)}) copy-start(f32[1,1,256]{2,1,0:T(1,128)} %copy-done.29) | copy-start | bytes 3076
  58.0 57.9 %copy-start.32 = (f32[1,1,256]{2,1,0:T(1,128)S(1)}, f32[1,1,256]{2,1,0:T(1,128)}, u32[]{:S(2)}) copy-start(f32[1,1,256]{2,1,0:T(1,128)} %copy-done.31) | copy-start | bytes 3076
  58.0 57.9 %copy-start.34 = (f32[1,1,256]{2,1,0:T(1,128)S(1)}, f32[1,1,256]{2,1,0:T(1,128)}, u32[]{:S(2)}) copy-start(f32[1,1,256]{2,1,0:T(1,128)} %copy-done.33) | copy-start | bytes 3076
  58.0 57.9 %copy-start.36 = (f32[1,1,256]{2,1,0:T(1,128)S(1)}, f32[1,1,256]{2,1,0:T(1,128)}, u32[]{:S(2)}) copy-start(f32[1,1,256]{2,1,0:T(1,128)} %copy-done.35) | copy-start | bytes 3076
  58.0 57.9 %copy-start.38 = (f32[1,1,256]{2,1,0:T(1,128)S(1)}, f32[1,1,256]{2,1,0:T(1,128)}, u32[]{:S(2)}) copy-start(f32[1,1,256]{2,1,0:T(1,128)} %copy-done.37) | copy-start | bytes 3076
  58.0 57.9 %copy-start.40 = (f32[1,1,256]{2,1,0:T(1,128)S(1)}, f32[1,1,256]{2,1,0:T(1,128)}, u32[]{:S(2)}) copy-start(f32[1,1,256]{2,1,0:T(1,128)} %copy-done.39) | copy-start | bytes 3076
  58.1 57.9 %copy-start.42 = (f32[1,1,256]{2,1,0:T(1,128)S(1)}, f32[1,1,256]{2,1,0:T(1,128)}, u32[]{:S(2)}) copy-start(f32[1,1,256]{2,1,0:T(1,128)} %copy-done.41) | copy-start | bytes 3076
  58.1 57.9 %copy-start.44 = (f32[1,1,256]{2,1,0:T(1,128)S(1)}, f32[1,1,256]{2,1,0:T(1,128)}, u32[]{:S(2)}) copy-start(f32[1,1,256]{2,1,0:T(1,128)} %copy-done.43) | copy-start | bytes 3076
  58.1 57.9 %copy-start.46 = (f32[1,1,256]{2,1,0:T(1,128)S(1)}, f32[1,1,256]{2,1,0:T(1,128)}, u32[]{:S(2)}) copy-start(f32[1,1,256]{2,1,0:T(1,128)} %copy-done.45) | copy-start | bytes 3076
  58.1 57.9 %copy-start.48 = (f32[1,1,256]{2,1,0:T(1,128)S(1)}, f32[1,1,256]{2,1,0:T(1,128)}, u32[]{:S(2)}) copy-start(f32[1,1,256]{2,1,0:T(1,128)} %copy-done.47) | copy-start | bytes 3076
  58.1 57.9 %copy-start.50 = (f32[1,1,256]{2,1,0:T(1,128)S(1)}, f32[1,1,256]{2,1,0:T(1,128)}, u32[]{:S(2)}) copy-start(f32[1,1,256]{2,1,0:T(1,128)} %copy-done.49) | copy-start | bytes 3076
  58.1 57.9 %copy-start.52 = (f32[1,1,256]{2,1,0:T(1,128)S(1)}, f32[1,1,256]{2,1,0:T(1,128)}, u32[]{:S(2)}) copy-start(f32[1,1,256]{2,1,0:T(1,128)} %copy-done.51) | copy-start | bytes 3076
  58.1 57.9 %copy-start.54 = (f32[1,1,256]{2,1,0:T(1,128)S(1)}, f32[1,1,256]{2,1,0:T(1,128)}, u32[]{:S(2)}) copy-start(f32[1,1,256]{2,1,0:T(1,128)} %copy-done.53) | copy-start | bytes 3076
  58.1 57.9 %copy-start.56 = (f32[1,1,256]{2,1,0:T(1,128)S(1)}, f32[1,1,256]{2,1,0:T(1,128)}, u32[]{:S(2)}) copy-start(f32[1,1,256]{2,1,0:T(1,128)} %copy-done.55) | copy-start | bytes 3076
  58.1 57.9 %copy-start.58 = (f32[1,1,256]{2,1,0:T(1,128)S(1)}, f32[1,1,256]{2,1,0:T(1,128)}, u32[]{:S(2)}) copy-start(f32[1,1,256]{2,1,0:T(1,128)} %copy-done.57) | copy-start | bytes 3076
  58.1 57.9 %copy-start.60 = (f32[1,1,256]{2,1,0:T(1,128)S(1)}, f32[1,1,256]{2,1,0:T(1,128)}, u32[]{:S(2)}) copy-start(f32[1,1,256]{2,1,0:T(1,128)} %copy-done.59) | copy-start | bytes 3076
  58.2 57.9 %copy-start.62 = (f32[1,1,256]{2,1,0:T(1,128)S(1)}, f32[1,1,256]{2,1,0:T(1,128)}, u32[]{:S(2)}) copy-start(f32[1,1,256]{2,1,0:T(1,128)} %copy-done.61) | copy-start | bytes 3076
  58.2 57.9 %copy-start.64 = (f32[1,1,256]{2,1,0:T(1,128)S(1)}, f32[1,1,256]{2,1,0:T(1,128)}, u32[]{:S(2)}) copy-start(f32[1,1,256]{2,1,0:T(1,128)} %copy-done.63) | copy-start | bytes 3076
  58.2 57.9 %copy-start.66 = (f32[1,1,256]{2,1,0:T(1,128)S(1)}, f32[1,1,256]{2,1,0:T(1,128)}, u32[]{:S(2)}) copy-start(f32[1,1,256]{2,1,0:T(1,128)} %copy-done.65) | copy-start | bytes 3076
  58.2 57.9 %copy-start.68 = (f32[1,1,256]{2,1,0:T(1,128)S(1)}, f32[1,1,256]{2,1,0:T(1,128)}, u32[]{:S(2)}) copy-start(f32[1,1,256]{2,1,0:T(1,128)} %copy-done.67) | copy-start | bytes 3076
  58.2 57.9 %copy-start.70 = (f32[1,1,256]{2,1,0:T(1,128)S(1)}, f32[1,1,256]{2,1,0:T(1,128)}, u32[]{:S(2)}) copy-start(f32[1,1,256]{2,1,0:T(1,128)} %copy-done.69) | copy-start | bytes 3076
  58.2 57.9 %copy-start.72 = (f32[1,1,256]{2,1,0:T(1,128)S(1)}, f32[1,1,256]{2,1,0:T(1,128)}, u32[]{:S(2)}) copy-start(f32[1,1,256]{2,1,0:T(1,128)} %copy-done.71) | copy-start | bytes 3076
  58.2 57.9 %copy-start.74 = (f32[1,1,256]{2,1,0:T(1,128)S(1)}, f32[1,1,256]{2,1,0:T(1,128)}, u32[]{:S(2)}) copy-start(f32[1,1,256]{2,1,0:T(1,128)} %copy-done.73) | copy-start | bytes 3076
  58.2 57.9 %copy-start.76 = (f32[1,1,256]{2,1,0:T(1,128)S(1)}, f32[1,1,256]{2,1,0:T(1,128)}, u32[]{:S(2)}) copy-start(f32[1,1,256]{2,1,0:T(1,128)} %copy-done.75) | copy-start | bytes 3076
  58.2 57.9 %copy-start.78 = (f32[1,1,256]{2,1,0:T(1,128)S(1)}, f32[1,1,256]{2,1,0:T(1,128)}, u32[]{:S(2)}) copy-start(f32[1,1,256]{2,1,0:T(1,128)} %copy-done.77) | copy-start | bytes 3076
  58.2 57.9 %copy-start.80 = (f32[1,1,256]{2,1,0:T(1,128)S(1)}, f32[1,1,256]{2,1,0:T(1,128)}, u32[]{:S(2)}) copy-start(f32[1,1,256]{2,1,0:T(1,128)} %copy-done.79) | copy-start | bytes 3076
  58.3 57.9 %copy-start.82 = (f32[1,1,256]{2,1,0:T(1,128)S(1)}, f32[1,1,256]{2,1,0:T(1,128)}, u32[]{:S(2)}) copy-start(f32[1,1,256]{2,1,0:T(1,128)} %copy-done.81) | copy-start | bytes 3076
  58.3 57.9 %copy-start.84 = (f32[1,1,256]{2,1,0:T(1,128)S(1)}, f32[1,1,256]{2,1,0:T(1,128)}, u32[]{:S(2)}) copy-start(f32[1,1,256]{2,1,0:T(1,128)} %copy-done.83) | copy-start | bytes 3076
  58.3 57.9 %copy-start.86 = (f32[1,1,256]{2,1,0:T(1,128)S(1)}, f32[1,1,256]{2,1,0:T(1,128)}, u32[]{:S(2)}) copy-start(f32[1,1,256]{2,1,0:T(1,128)} %copy-done.85) | copy-start | bytes 3076
  58.3 57.9 %copy-start.88 = (f32[1,1,256]{2,1,0:T(1,128)S(1)}, f32[1,1,256]{2,1,0:T(1,128)}, u32[]{:S(2)}) copy-start(f32[1,1,256]{2,1,0:T(1,128)} %copy-done.87) | copy-start | bytes 3076
  58.3 57.9 %copy-start.90 = (f32[1,1,256]{2,1,0:T(1,128)S(1)}, f32[1,1,256]{2,1,0:T(1,128)}, u32[]{:S(2)}) copy-start(f32[1,1,256]{2,1,0:T(1,128)} %copy-done.89) | copy-start | bytes 3076
  58.3 57.9 %copy-start.92 = (f32[1,1,256]{2,1,0:T(1,128)S(1)}, f32[1,1,256]{2,1,0:T(1,128)}, u32[]{:S(2)}) copy-start(f32[1,1,256]{2,1,0:T(1,128)} %copy-done.91) | copy-start | bytes 3076
  61.3 44.3 %collective-permute-start.4 = (bf16[1,32,3,256]{3,2,1,0:T(4,128)(2,1)S(1)}, bf16[1,32,3,256]{3,2,1,0:T(4,128)(2,1)S(1)}, u32[]{:S(2)}, u32[]{:S(2)}) collective-permute-start(bf16[1,32,3,256]{3,2,1,0:T(4,128)(2,1)S(1)} %get-tuple-element.76), channel_id=1, source_target_pairs={{0,2},{2,4},{4,6},{6,8},{8,10},{10,12},{12,14},{14,16},{16,18},{18... | collective-permute-start | bytes 147464 | tf_op jit(solution)/shard_map/ppermute | solution.py:23
  61.4 44.2 %collective-permute-start.5 = (bf16[1,32,3,256]{3,2,1,0:T(4,128)(2,1)S(1)}, bf16[1,32,3,256]{3,2,1,0:T(4,128)(2,1)S(1)}, u32[]{:S(2)}, u32[]{:S(2)}) collective-permute-start(bf16[1,32,3,256]{3,2,1,0:T(4,128)(2,1)S(1)} %get-tuple-element.77), channel_id=1, source_target_pairs={{2,0},{4,2},{6,4},{8,6},{10,8},{12,10},{14,12},{16,14},{18,16},{20... | collective-permute-start | bytes 147464 | tf_op jit(solution)/shard_map/ppermute | solution.py:25
  105.6 7.4 %collective-permute-start.6 = (bf16[1,3,22,256]{3,2,1,0:T(8,128)(2,1)S(1)}, bf16[1,3,22,256]{3,2,1,0:T(8,128)(2,1)S(1)}, u32[]{:S(2)}, u32[]{:S(2)}) collective-permute-start(bf16[1,3,22,256]{3,2,1,0:T(8,128)(2,1)S(1)} %get-tuple-element.72), channel_id=1, source_target_pairs={{0,1},{2,3},{4,5},{6,7},{8,9},{10,11},{12,13},{14,15},{16,17},{18,... | collective-permute-start | bytes 101384 | tf_op jit(solution)/shard_map/ppermute | solution.py:23
  109.8 5.9 %collective-permute-start.7 = (bf16[1,3,22,256]{3,2,1,0:T(8,128)(2,1)S(1)}, bf16[1,3,22,256]{3,2,1,0:T(8,128)(2,1)S(1)}, u32[]{:S(2)}, u32[]{:S(2)}) collective-permute-start(bf16[1,3,22,256]{3,2,1,0:T(8,128)(2,1)S(1)} %get-tuple-element.73), channel_id=1, source_target_pairs={{1,0},{3,2},{5,4},{7,6},{9,8},{11,10},{13,12},{15,14},{17,16},{19,... | collective-permute-start | bytes 101384 | tf_op jit(solution)/shard_map/ppermute | solution.py:25
  (60 other events, 651.4 us)
Sparse Core Ops, SparseCore 0:
  57.3 143.0 all-reduce.3
where the time goes:
time: 221 us
  waiting for transfers between devices  83.1 us (38%)
  blocking collectives  38.1 us (17%)
  other arithmetic  29.6 us (13%)
  starting transfers between devices  20.6 us (9%)
  between operations  19.6 us (9%)
  matrix products  16.1 us (7%)
  local copies, waits for them, and re-layouts  13.5 us (6%)
    psum x1, waiting for transfers between devices, body(): lax.psum((raw_kernel, unclipped_gain, raw_inner, raw_outer, raw_scale), (...  79.2 us
    psum x1, blocking collectives, body(): lax.psum((raw_kernel, unclipped_gain, raw_inner, raw_outer, raw_scale), (...  38.1 us
    ppermute x4, starting transfers between devices, padded_2(): lax.ppermute(head, axis, [((i + 1) % count, i) for i in range(ends)])  12.1 us
    ppermute x4, starting transfers between devices, padded_2(): lax.ppermute(tail, axis, [(i, (i + 1) % count) for i in range(ends)])  8.5 us
    dot_general x1, matrix products, body(): jnp.dot(normalized_output, inner_weight, preferred_element_type=jnp.float32)  5.79 us
    convert_element_type x1, other arithmetic, body(): (grad_blocked.reshape(field.shape).astype(jnp.float32) + spread).astype(j...  5.07 us
    reduce_sum x3, other arithmetic, kernel_terms(): jnp.sum(padded[:, row_shift:row_shift + rows, col_shift:col_shift + cols]...  4.77 us
    reduce_sum x1, other arithmetic, body(): centered_input = mixed - jnp.mean(mixed, axis=-1, keepdims=True)  4.53 us
  transfers between devices with their start and end apart: 9, of which 3 were waited for; matrix products, arithmetic and copies ran while one was open for 8% of the time, Pallas kernels for 0%

commit v1 on v0

--- a/solution.py
+++ b/solution.py
@@ -4,6 +4,8 @@
 import jax
 import jax.numpy as jnp
 from jax import lax
+from jax.experimental import pallas as pl
+from jax.experimental.pallas import tpu as pltpu
 from jax.sharding import PartitionSpec as P
 
 PARAMS = 1061632
@@ -92,11 +94,227 @@
     )
 
 
-def reduce_down(raw_down):
-    return lax.psum(raw_down, ("lon", "lat"))
+MESH = pl.DeviceIdType.MESH
+
+
+def place(mesh_shape):
+    lon_bits = mesh_shape["lon"].bit_length() - 1
+    lat_bits = mesh_shape["lat"].bit_length() - 1
+    core = ("lon", 0)
+    groups = [
+        [("lat", k) for k in range(lat_bits)],
+        [("lon", k) for k in range(1, min(2, lon_bits))],
+        [("lon", k) for k in range(2, lon_bits)],
+    ]
+    orders = []
+    for p in range(3):
+        rotated = groups[p:] + groups[:p]
+        orders.append([core] + [bit for group in rotated for bit in group])
+    devices = mesh_shape["lon"] * mesh_shape["lat"]
+    unit = 3 * 16 * devices
+    rows = -(-(4096 + 64) // unit) * unit
+    return orders, rows, devices
+
+
+def partner_of(bit):
+    axis, k = bit
+    me = lax.axis_index(axis)
+    b = lax.rem(lax.div(me, 2**k), 2)
+    return b, {axis: me + (1 - 2 * b) * 2**k}
+
+
+def sum_kernel_body(orders, devices, inner, outer, down, small, out, acc, send, recv, ssem, rsem):
+    rows = acc.shape[0]
+    part_rows = rows // 3
+    stages = len(orders[0])
+    barrier = pltpu.get_barrier_semaphore()
+    for bit in orders[0]:
+        _, device = partner_of(bit)
+        pl.semaphore_signal(barrier, inc=1, device_id=device, device_id_type=MESH)
+
+    def pack_inner(i, carry):
+        r = pl.multiple_of(i * 64, 64)
+        for c in range(4):
+            acc[pl.ds(c * 256 + r, 64), :] = inner[pl.ds(r, 64), c * 256 : (c + 1) * 256]
+        return carry
+
+    lax.fori_loop(0, 4, pack_inner, 0)
+
+    def pack_rest(i, carry):
+        r = pl.multiple_of(i * 64, 64)
+        acc[pl.ds(1024 + r, 64), :] = outer[pl.ds(r, 64), :]
+        acc[pl.ds(2048 + r, 64), :] = down[pl.ds(r, 64), 0:256]
+        acc[pl.ds(3072 + r, 64), :] = down[pl.ds(r, 64), 256:512]
+        return carry
+
+    lax.fori_loop(0, 16, pack_rest, 0)
+    acc[4096:4160, :] = small[...]
+
+    def clear(i, carry):
+        acc[pl.ds(pl.multiple_of(4160 + i * 32, 32), 32), :] = jnp.zeros((32, 256), jnp.float32)
+        return carry
+
+    lax.fori_loop(0, (rows - 4160) // 32, clear, 0)
+    pl.semaphore_wait(barrier, stages)
+
+    unit = part_rows // devices
+    offs = [p * part_rows for p in range(3)]
+    keeps = [[None] * stages for _ in range(3)]
+    sent = []
+
+    def start(s, p):
+        b, device = partner_of(orders[p][s])
+        half = part_rows >> (s + 1)
+        base = p * part_rows + part_rows - 2 * half
+        away = offs[p] + (1 - b) * half
+        keeps[p][s] = offs[p] + b * half
+        chunk = min(half, 4 * unit)
+
+        def cast(i, carry):
+            r = i * chunk
+            send[pl.ds(pl.multiple_of(base + r, 16), chunk), :] = acc[
+                pl.ds(pl.multiple_of(away + r, 16), chunk), :
+            ].astype(jnp.bfloat16)
+            return carry
+
+        lax.fori_loop(0, half // chunk, cast, 0)
+        copy = pltpu.make_async_remote_copy(
+            src_ref=send.at[pl.ds(base, half)],
+            dst_ref=recv.at[pl.ds(base, half)],
+            send_sem=ssem.at[p, s],
+            recv_sem=rsem.at[p, s],
+            device_id=device,
+            device_id_type=MESH,
+        )
+        copy.start()
+        sent.append(copy)
+        return copy
+
+    def finish(s, p, copy):
+        half = part_rows >> (s + 1)
+        base = p * part_rows + part_rows - 2 * half
+        keep = keeps[p][s]
+        chunk = min(half, 4 * unit)
+        copy.wait_recv()
+
+        def add(i, carry):
+            r = i * chunk
+            mine = pl.ds(pl.multiple_of(keep + r, 16), chunk)
+            acc[mine, :] = acc[mine, :] + recv[
+                pl.ds(pl.multiple_of(base + r, 16), chunk), :
+            ].astype(jnp.float32)
+            return carry
+
+        lax.fori_loop(0, half // chunk, add, 0)
+        offs[p] = keep
+
+    def spread(s, p):
+        _, device = partner_of(orders[p][s])
+        half = part_rows >> (s + 1)
+        mine = pl.ds(pl.multiple_of(keeps[p][s], 16), half)
+        copy = pltpu.make_async_remote_copy(
+            src_ref=out.at[mine],
+            dst_ref=out.at[mine],
+            send_sem=ssem.at[p, stages + s],
+            recv_sem=rsem.at[p, stages + s],
+            device_id=device,
+            device_id_type=MESH,
+        )
+        copy.start()
+        sent.append(copy)
+        return copy
+
+    flight = [start(0, p) for p in range(3)]
+    for s in range(stages):
+        for p in range(3):
+            finish(s, p, flight[p])
+            if s + 1 < stages:
+                flight[p] = start(s + 1, p)
+            else:
+                mine = pl.ds(pl.multiple_of(offs[p], 16), unit)
+                out[mine, :] = acc[mine, :].astype(jnp.bfloat16)
+                flight[p] = spread(stages - 1, p)
+    for s in range(stages - 2, -1, -1):
+        for p in range(3):
+            flight[p].wait_recv()
+            flight[p] = spread(s, p)
+    for p in range(3):
+        flight[p].wait_recv()
+    for copy in sent:
+        copy.wait_send()
+
+
+def summed(inner, outer, down, small, mesh_shape):
+    orders, rows, devices = place(mesh_shape)
+    stages = len(orders[0])
+    vmem = pl.BlockSpec(memory_space=pltpu.VMEM)
+    return pl.pallas_call(
+        partial(sum_kernel_body, orders, devices),
+        name="sum_gradients",
+        out_shape=jax.ShapeDtypeStruct((rows, 256), jnp.bfloat16),
+        in_specs=[vmem] * 4,
+        out_specs=vmem,
+        scratch_shapes=[
+            pltpu.VMEM((rows, 256), jnp.float32),
+            pltpu.VMEM((rows, 256), jnp.bfloat16),
+            pltpu.VMEM((rows, 256), jnp.bfloat16),
+            pltpu.SemaphoreType.DMA((3, 2 * stages)),
+            pltpu.SemaphoreType.DMA((3, 2 * stages)),
+        ],
+        compiler_params=pltpu.CompilerParams(
+            collective_id=1, has_side_effects=True, vmem_limit_bytes=48 << 20
+        ),
+    )(inner, outer, down, small)
+
+
+def clip_body(sums, inner, outer, down, small):
+    def squares(i, total):
+        v = sums[pl.ds(pl.multiple_of(i * 64, 64), 64), :].astype(jnp.float32)
+        v = v * v
+        for width in (32, 16, 8):
+            v = v[:width] + v[width:]
+        return total + v
+
+    total = jnp.sum(lax.fori_loop(0, 65, squares, jnp.zeros((8, 256), jnp.float32)))
+    total = jnp.full((1, 256), total, jnp.float32)
+    factor = jnp.minimum(1.0, math.sqrt(PARAMS) / jnp.sqrt(total + EPS))
+
+    def write_inner(i, carry):
+        r = pl.multiple_of(i * 64, 64)
+        for c in range(4):
+            inner[pl.ds(r, 64), c * 256 : (c + 1) * 256] = (
+                sums[pl.ds(c * 256 + r, 64), :].astype(jnp.float32) * factor
+            )
+        return carry
+
+    lax.fori_loop(0, 4, write_inner, 0)
+
+    def write_rest(i, carry):
+        r = pl.multiple_of(i * 64, 64)
+        outer[pl.ds(r, 64), :] = sums[pl.ds(1024 + r, 64), :].astype(jnp.float32) * factor
+        down[pl.ds(r, 64), 0:256] = sums[pl.ds(2048 + r, 64), :].astype(jnp.float32) * factor
+        down[pl.ds(r, 64), 256:512] = sums[pl.ds(3072 + r, 64), :].astype(jnp.float32) * factor
+        return carry
+
+    lax.fori_loop(0, 16, write_rest, 0)
+    small[...] = sums[4096:4160, :].astype(jnp.float32) * factor
+
+
+def clipped(sums):
+    vmem = pl.BlockSpec(memory_space=pltpu.VMEM)
+    shapes = ((256, 1024), (1024, 256), (1024, 512), (64, 256))
+    return pl.pallas_call(
+        clip_body,
+        name="clip_gradients",
+        out_shape=[jax.ShapeDtypeStruct(shape, jnp.float32) for shape in shapes],
+        in_specs=[vmem],
+        out_specs=[vmem] * 4,
+        compiler_params=pltpu.CompilerParams(vmem_limit_bytes=48 << 20),
+    )(sums)
 
 
 def body(
+    mesh_shape,
     field,
     depth_kernel,
     layer_norm_gain,
@@ -160,26 +378,19 @@
         jnp.bfloat16
     )
     raw_kernel = kernel_terms(padded.astype(jnp.float32), depthwise_gradient.astype(jnp.float32))
-    summed_down = reduce_down(raw_down)
-    limit = math.sqrt(PARAMS)
-    sum_kernel, sum_gain, sum_inner, sum_outer, sum_scale = lax.psum(
-        (raw_kernel, unclipped_gain, raw_inner, raw_outer, raw_scale), ("lon", "lat")
-    )
-    total = (
-        jnp.sum(sum_kernel * sum_kernel)
-        + jnp.sum(sum_gain * sum_gain)
-        + jnp.sum(sum_inner * sum_inner)
-        + jnp.sum(sum_outer * sum_outer)
-        + jnp.sum(sum_scale * sum_scale)
-        + jnp.sum(summed_down * summed_down)
-    )
-    factor = jnp.minimum(1.0, limit / jnp.sqrt(total + EPS))
-    grad_kernel = sum_kernel * factor
-    grad_gain = sum_gain * factor
-    grad_inner = sum_inner * factor
-    grad_outer = sum_outer * factor
-    grad_scale = sum_scale * factor
-    grad_down = summed_down * factor
+    small = jnp.concatenate(
+        [
+            raw_kernel.reshape(49, channel_count),
+            unclipped_gain[None],
+            raw_scale[None],
+            jnp.zeros((13, channel_count), jnp.float32),
+        ]
+    )
+    sums = summed(raw_inner, raw_outer, raw_down, small, mesh_shape)
+    grad_inner, grad_outer, grad_down, grad_small = clipped(sums)
+    grad_kernel = grad_small[:49].reshape(7, 7, channel_count)
+    grad_gain = grad_small[49]
+    grad_scale = grad_small[50]
     return (
         coarse,
         grad_field,
@@ -194,7 +405,7 @@
 
 def solution(mesh):
     return jax.shard_map(
-        body,
+        partial(body, dict(mesh.shape)),
         mesh=mesh,
         in_specs=(
             P(None, "lat", "lon", None),

time: 221 us -> 131 us (0.59)
  waiting for transfers between devices: 83.1 us -> 5.57 us
  Pallas kernels: 0 us -> 48.5 us
  blocking collectives: 38.1 us -> 0 us
  between operations: 19.6 us -> 2.21 us
  other arithmetic: 29.6 us -> 18.8 us
  local copies, waits for them, and re-layouts: 13.5 us -> 21.3 us
    psum x1 -> x0, waiting for transfers between devices: 79.2 us -> none  [body(): lax.psum((raw_kernel, unclipped_gain, raw_inner, raw_outer, raw_scale), (...]
    pallas_call x0 -> x2, Pallas kernels: none -> 48.5 us  [the longest x1 45.3 us: summed(): pl.pallas_call(partial(sum_kernel_body, orders, devices), name='sum_gradi...]
    psum x1 -> x0, blocking collectives: 38.1 us -> none  [body(): lax.psum((raw_kernel, unclipped_gain, raw_inner, raw_outer, raw_scale), (...]
    reduce_sum x5 -> x0, other arithmetic: 5.9 us -> none  [the longest x1 2.88 us: body(): jnp.sum(summed_down * summed_down)]
    mul x6 -> x0, other arithmetic: 5.42 us -> none  [the longest x1 1.54 us: body(): grad_down = summed_down * factor]
    concatenate x0 -> x1, local copies, waits for them, and re-layouts: none -> 5.14 us  [body(): jnp.concatenate([raw_kernel.reshape(49, channel_count), unclipped_gain[No...]
    unnamed x198 -> x208, local copies, waits for them, and re-layouts: 1.36 us -> 5.99 us
    another operation x1 -> x0, local copies, waits for them, and re-layouts: 2.92 us -> none  [kernel_terms(): return jnp.stack(terms).reshape(7, 7, grad.shape[3])]
  transfers between devices with their start and end apart: 9 -> 8, of which waited for: 3 -> 3; matrix products, arithmetic and copies ran while one was open for 8% -> 7% of each run, Pallas kernels for 0% -> 0%
where the time goes in v1:
time: 131 us; the launch traced here: 130 us
  Pallas kernels  48.5 us (37%)
  local copies, waits for them, and re-layouts  21.3 us (16%)
  other arithmetic  18.8 us (14%)
  starting transfers between devices  18.5 us (14%)
  matrix products  14.9 us (11%)
  waiting for transfers between devices  5.57 us (4%)
  between operations  2.21 us (2%)
    pallas_call x1, Pallas kernels, summed(): pl.pallas_call(partial(sum_kernel_body, orders, devices), name='sum_gradi...  45.3 us
    ppermute x4, starting transfers between devices, padded_2(): lax.ppermute(head, axis, [((i + 1) % count, i) for i in range(ends)])  11.7 us
    ppermute x4, starting transfers between devices, padded_2(): lax.ppermute(tail, axis, [(i, (i + 1) % count) for i in range(ends)])  6.82 us
    unnamed x208, local copies, waits for them, and re-layouts  5.99 us
    reduce_sum x3, other arithmetic, kernel_terms(): jnp.sum(padded[:, row_shift:row_shift + rows, col_shift:col_shift + cols]...  5.97 us
    dot_general x1, matrix products, body(): jnp.dot(normalized_output, inner_weight, preferred_element_type=jnp.float32)  5.62 us
    concatenate x1, local copies, waits for them, and re-layouts, body(): jnp.concatenate([raw_kernel.reshape(49, channel_count), unclipped_gain[No...  5.14 us
    convert_element_type x1, other arithmetic, body(): (grad_blocked.reshape(field.shape).astype(jnp.float32) + spread).astype(j...  5.08 us
  transfers between devices with their start and end apart: 8, of which 3 were waited for; matrix products, arithmetic and copies ran while one was open for 7% of the time, Pallas kernels for 0%

profile of v1, /device:TPU:0, one launch (start us, length us, event | category | flops | bytes accessed | tf_op | source)
XLA Modules:
  0.0 129.8 jit_solution(14598238029820642501)
XLA Ops:
  0.6 1.1 fusion.114
  1.8 0.5 collective-permute-start
  2.3 5.1 %collective-permute-start.1 = (bf16[1,32,3,256]{3,2,1,0:T(4,128)(2,1)S(1)}, bf16[1,32,3,256]{3,2,1,0:T(4,128)(2,1)S(1)}, u32[]{:S(2)}, u32[]{:S(2)}) collective-permute-start(bf16[1,32,3,256]{3,2,1,0:T(4,128)(2,1)S(1)} %get-tuple-element.81), channel_id=1, source_target_pairs={{2,0},{4,2},{6,4},{8,6},{10,8},{12,10},{14,12},{16,14},{18,16},{20... | collective-permute-start | bytes 147464 | tf_op jit(solution)/shard_map/ppermute | solution.py:27
  7.3 1.0 fusion.116
  8.5 1.4 %convolution_convert_fusion = bf16[128,1024]{1,0:T(8,128)(2,1)S(1)} fusion(bf16[1024,512]{1,0:T(8,128)(2,1)S(1)} %copy-done, bf16[1,16,8,512]{3,2,1,0:T(8,128)(2,1)} %param.15), kind=kOutput, calls=%fused_computation.66 | convolution fusion | flops 134348800 | bytes 1441792 | tf_op jit(solution)/shard_map/dot_general | solution.py:350
  9.9 1.0 fusion.117
  11.2 0.8 pad_maximum_fusion.5
  12.0 3.8 %collective-permute-start.2 = (bf16[1,3,22,256]{3,2,1,0:T(8,128)(2,1)S(1)}, bf16[1,3,22,256]{3,2,1,0:T(8,128)(2,1)S(1)}, u32[]{:S(2)}, u32[]{:S(2)}) collective-permute-start(bf16[1,3,22,256]{3,2,1,0:T(8,128)(2,1)S(1)} %get-tuple-element.76), channel_id=1, source_target_pairs={{0,1},{2,3},{4,5},{6,7},{8,9},{10,11},{12,13},{14,15},{16,17},{18,... | collective-permute-start | bytes 101384 | tf_op jit(solution)/shard_map/ppermute | solution.py:25
  15.8 1.3 collective-permute-start.3
  17.1 1.5 %fusion.118 = (f32[1,1,256]{2,1,0:T(1,128)}, f32[1,1,256]{2,1,0:T(1,128)}, f32[1,1,256]{2,1,0:T(1,128)}, f32[1,1,256]{2,1,0:T(1,128)}, f32[1,1,256]{2,1,0:T(1,12...) fusion(f32[7,7,256]{2,1,0:T(8,128)} %param.9), kind=kLoop, calls=%fused_computation.253 | loop fusion | bytes 22528 | tf_op jit(solution)/shard_map/slice | solution.py:42
  18.8 0.4 reshape.367
  19.2 1.2 reshape.366
  20.4 1.3 collective-permute-done.3
  22.2 4.7 %fusion.112 = (f32[32,16]{1,0:T(8,128)S(1)}, f32[1,32,16,256]{3,2,1,0:T(8,128)S(1)}) fusion(f32[1,38,22,256]{3,2,1,0:T(8,128)S(1)} %maximum_convert_fusion, f32[256]{0:T(256)} %bitcast.49, f32[256]{0:T(256)} %bitcast.48, f32[256]{0:T(256)S(1)} %bitcast.148, f32[256]{0:T(256)S(1)} %bitcast.150, f32[256]{0:T(256)S(1)} %bitcast.152, f32[256]{0:T(256)S(1)} %bitcast.154, ...), kind=kLoop, calls=%fused_computation.247 | loop fusion | flops 12844544 | bytes 26266624 | tf_op jit(solution)/shard_map/reduce_sum | solution.py:331
  27.0 0.2 multiply_reduce_fusion.4
  27.5 5.6 %multiply_convert_fusion = (bf16[512,1024]{1,0:T(8,128)(2,1)}, f32[512,1024]{1,0:T(8,128)S(1)}, f32[512,1024]{1,0:T(8,128)S(1)}) fusion(bf16[512,256]{1,0:T(8,128)(2,1)S(1)} %bitcast.142, bf16[256,1024]{1,0:T(8,128)(2,1)S(1)} %copy-done.103), kind=kOutput, calls=%fused_computation.52 | convolution fusion | flops 302514176 | bytes 6029312 | tf_op jit(solution)/shard_map/dot_general | solution.py:339
  33.1 1.0 add_convert_fusion
  34.2 1.0 copy-done.11
  35.1 0.6 multiply_reduce_fusion.3
  35.7 0.8 multiply_reduce_fusion.1
  36.5 0.6 broadcast_multiply_fusion
  37.1 0.7 div.17
  37.8 3.0 %fusion.54 = (f32[256]{0:T(256)}, f32[256]{0:T(256)}, f32[256]{0:T(256)}, f32[256]{0:T(256)}, f32[256]{0:T(256)}, /*index=5*/f32[256]{0:T(256)}, f32[256]{0:T(25...) fusion(f32[1,38,22,256]{3,2,1,0:T(8,128)S(1)} %maximum_convert_, ...), kind=kLoop, calls=%fused_computation.116 | loop fusion | flops 5893632 | bytes 10775552 | tf_op jit(solution)/shard_map/reduce_sum | solution.py:71
  40.8 1.7 %fusion.55 = (f32[256]{0:T(256)}, f32[256]{0:T(256)}, f32[256]{0:T(256)}, f32[256]{0:T(256)}, f32[256]{0:T(256)}, /*index=5*/f32[256]{0:T(256)}, f32[256]{0:T(25...) fusion(bf16[1,32,16,256]{3,2,1,0:T(8,128)(2,1)S(1)} %get-tuple-, ...), kind=kLoop, calls=%fused_computation.117 | loop fusion | flops 4845056 | bytes 9717760 | tf_op jit(solution)/shard_map/reduce_sum | solution.py:71
  42.5 1.3 %fusion.53 = (f32[256]{0:T(256)}, f32[256]{0:T(256)}, f32[256]{0:T(256)}, f32[256]{0:T(256)}, f32[256]{0:T(256)}, /*index=5*/f32[256]{0:T(256)}, f32[256]{0:T(25...) fusion(bf16[1,32,16,256]{3,2,1,0:T(8,128)(2,1)S(1)} %get-tuple-element.67, ...), kind=kLoop, calls=%fused_computation.115 | loop fusion | flops 3535616 | bytes 7091200 | tf_op jit(solution)/shard_map/reduce_sum | solution.py:71
  43.8 1.4 %fusion.119.inner = f32[256,1024]{1,0:T(8,128)} fusion(bf16[512,256]{1,0:T(8,128)(2,1)S(1)} %bitcast.143, bf16[512,1024]{1,0:T(8,128)(2,1)S(1)} %copy-done.12), kind=kOutput, calls=%fused_computation.254 | convolution fusion | flops 268435456 | bytes 2359296 | tf_op jit(solution)/shard_map/dot_general | solution.py:361
  45.3 0.5 copy-done.14
  45.7 1.0 multiply_reduce_fusion
  46.8 1.5 %fusion.110.outer = f32[1024,256]{1,0:T(8,128)} fusion(bf16[512,1024]{1,0:T(8,128)(2,1)S(1)} %copy-done.6, f32[512,256]{1,0:T(8,128)S(1)} %copy-done.5, f32[256]{0:T(256)S(1)} %copy-done.98), kind=kOutput, calls=%fused_computation.236 | convolution fusion | flops 268697600 | bytes 2622464 | tf_op jit(solution)/shard_map/dot_general | solution.py:360
  48.2 0.7 fusion.113
  49.3 0.9 reshape.359
  50.1 1.4 %fusion.107.down = f32[1024,512]{1,0:T(8,128)S(1)} fusion(bf16[128,1024]{1,0:T(8,128)(2,1)} %reshape.359, bf16[1,16,8,512]{3,2,1,0:T(8,128)(2,1)S(1)} %copy-done.15), kind=kOutput, calls=%fused_computation.233 | convolution fusion | flops 134217728 | bytes 2490368 | tf_op jit(solution)/shard_map/dot_general | solution.py:349
  51.6 5.1 %concatenate.35.small = f32[64,256]{1,0:T(8,128)S(1)} concatenate(f32[1,256]{1,0:T(1,128)} %bitcast.253, f32[1,256]{1,0:T(1,128)} %bitcast.256, f32[1,256]{1,0:T(1,128)} %bitcast.257, f32[1,256]{1,0:T(1,128)} %bitcast.258, f32[1,256]{1,0:T(1,128)} %bitcast.259, f32[1,256]{1,0:T(1,128)} %bitcast.260, f32[1,256]{1,0:T(1,128)} %bitcast.261, f32[1,256]{1,0:T(1,128)} %bitcast.262, ...), dimensions={0} | concatenate | bytes 131072 | tf_op jit(solution)/shard_map/concatenate | solution.py:381
  56.8 1.2 copy-done.2
  58.0 1.2 copy-done.3
  59.2 45.3 %sum_gradients.1.sums = bf16[4608,256]{1,0:T(8,128)(2,1)} custom-call(f32[256,1024]{1,0:T(8,128)S(1)} %copy-done.3, f32[1024,256]{1,0:T(8,128)S(1)} %copy-done.2, f32[1024,512]{1,0:T(8,128)S(1)} %fusion.107.down, f32[64,256]{1,0:T(8,128)S(1)} %concatenate.35.small), custom_call_target="tpu_custom_call" | custom-call | tf_op jit(solution)/shard_map/sum_gradients/pallas_call | solution.py:251
  104.5 1.7 %copy-done.1 = bf16[4608,256]{1,0:T(8,128)(2,1)S(1)} copy-done((bf16[4608,256]{1,0:T(8,128)(2,1)S(1)}, bf16[4608,256]{1,0:T(8,128)(2,1)}, u32[]{:S(2)}) %copy-start.1) | copy-done | bytes 2359320
  106.2 3.2 %clip_gradients.1 = (f32[256,1024]{1,0:T(8,128)}, f32[1024,256]{1,0:T(8,128)}, f32[1024,512]{1,0:T(8,128)}, f32[64,256]{1,0:T(8,128)S(1)}) custom-call(bf16[4608,256]{1,0:T(8,128)(2,1)S(1)} %copy-done.1), custom_call_target="tpu_custom_call" | custom-call | tf_op jit(solution)/shard_map/clip_gradients/pallas_call | solution.py:306
  109.7 0.5 collective-permute-start.4
  110.2 4.0 %collective-permute-start.5 = (bf16[1,32,3,256]{3,2,1,0:T(4,128)(2,1)S(1)}, bf16[1,32,3,256]{3,2,1,0:T(4,128)(2,1)S(1)}, u32[]{:S(2)}, u32[]{:S(2)}) collective-permute-start(bf16[1,32,3,256]{3,2,1,0:T(4,128)(2,1)S(1)} %copy-done.18), channel_id=1, source_target_pairs={{2,0},{4,2},{6,4},{8,6},{10,8},{12,10},{14,12},{16,14},{18,16},{20... | collective-permute-start | bytes 147464 | tf_op jit(solution)/shard_map/ppermute | solution.py:27
  114.2 0.6 fusion.115
  114.8 1.4 %collective-permute-done.4 = bf16[1,32,3,256]{3,2,1,0:T(4,128)(2,1)S(1)} collective-permute-done((bf16[1,32,3,256]{3,2,1,0:T(4,128)(2,1)S(1)}, bf16[1,32,3,256]{3,2,1,0:T(4,128)(2,1)S(1)}, u32[]{:S(2)}, u32[]{:S(2)}) %collective-permute-start.4) | collective-permute-done | bytes 49184 | tf_op jit(solution)/shard_map/ppermute | solution.py:25
  116.2 2.1 %collective-permute-start.6 = (bf16[1,3,22,256]{3,2,1,0:T(8,128)(2,1)S(1)}, bf16[1,3,22,256]{3,2,1,0:T(8,128)(2,1)S(1)}, u32[]{:S(2)}, u32[]{:S(2)}) collective-permute-start(bf16[1,3,22,256]{3,2,1,0:T(8,128)(2,1)S(1)} %get-tuple-element.74), channel_id=1, source_target_pairs={{0,1},{2,3},{4,5},{6,7},{8,9},{10,11},{12,13},{14,15},{16,17},{18,... | collective-permute-start | bytes 101384 | tf_op jit(solution)/shard_map/ppermute | solution.py:25
  118.3 1.3 collective-permute-start.7
  119.6 1.0 fusion.6
  120.6 0.6 reshape.363
  121.2 2.9 %collective-permute-done.7 = bf16[1,3,22,256]{3,2,1,0:T(8,128)(2,1)S(1)} collective-permute-done((bf16[1,3,22,256]{3,2,1,0:T(8,128)(2,1)S(1)}, bf16[1,3,22,256]{3,2,1,0:T(8,128)(2,1)S(1)}, u32[]{:S(2)}, u32[]{:S(2)}) %collective-permute-start.7) | collective-permute-done | bytes 33824 | tf_op jit(solution)/shard_map/ppermute | solution.py:27
  124.7 5.1 %fusion.58 = bf16[1,32,16,256]{3,2,1,0:T(8,128)(2,1)} fusion(f32[1,32,16,256]{3,2,1,0:T(8,128)S(1)} %copy-done.10, f32[1,38,22,256]{3,2,1,0:T(8,128)S(1)} %maximum_convert_fusion.1, f32[256]{0:T(256)} %bitcast.49, f32[256]{0:T(256)} %bitcast.48, f32[256]{0:T(256)S(1)} %bitcast.149, f32[256]{0:T(256)S(1)} %bitcast.151, f32[256]{0:T(256)S(1)} %bitcast.153, ...), kind=kLoop, calls=%fused_computation.121 | loop fusion | flops 12976128 | bytes 26526720 | tf_op jit(solution)/shard_map/convert_element_type | solution.py:377
  (220 shorter events, 1.6 us)
Async XLA Ops:
  1.8 9.4 %collective-permute-start = (bf16[1,32,3,256]{3,2,1,0:T(4,128)(2,1)S(1)}, bf16[1,32,3,256]{3,2,1,0:T(4,128)(2,1)S(1)}, u32[]{:S(2)}, u32[]{:S(2)}) collective-permute-start(bf16[1,32,3,256]{3,2,1,0:T(4,128)(2,1)S(1)} %get-tuple-element.80), channel_id=1, source_target_pairs={{0,2},{2,4},{4,6},{6,8},{8,10},{10,12},{12,14},{14,16},{16,18},{18... | collective-permute-start | bytes 147464 | tf_op jit(solution)/shard_map/ppermute | solution.py:25
  2.3 8.9 %collective-permute-start.1 = (bf16[1,32,3,256]{3,2,1,0:T(4,128)(2,1)S(1)}, bf16[1,32,3,256]{3,2,1,0:T(4,128)(2,1)S(1)}, u32[]{:S(2)}, u32[]{:S(2)}) collective-permute-start(bf16[1,32,3,256]{3,2,1,0:T(4,128)(2,1)S(1)} %get-tuple-element.81), channel_id=1, source_target_pairs={{2,0},{4,2},{6,4},{8,6},{10,8},{12,10},{14,12},{16,14},{18,16},{20... | collective-permute-start | bytes 147464 | tf_op jit(solution)/shard_map/ppermute | solution.py:27
  8.3 13.5 %copy-start.21 = (f32[1,1,256]{2,1,0:T(1,128)}, f32[1,1,256]{2,1,0:T(1,128)S(1)}, u32[]{:S(2)}) copy-start(f32[1,1,256]{2,1,0:T(1,128)S(1)} %get-tuple-element.84) | copy-start | bytes 3076
  12.0 8.4 %collective-permute-start.2 = (bf16[1,3,22,256]{3,2,1,0:T(8,128)(2,1)S(1)}, bf16[1,3,22,256]{3,2,1,0:T(8,128)(2,1)S(1)}, u32[]{:S(2)}, u32[]{:S(2)}) collective-permute-start(bf16[1,3,22,256]{3,2,1,0:T(8,128)(2,1)S(1)} %get-tuple-element.76), channel_id=1, source_target_pairs={{0,1},{2,3},{4,5},{6,7},{8,9},{10,11},{12,13},{14,15},{16,17},{18,... | collective-permute-start | bytes 101384 | tf_op jit(solution)/shard_map/ppermute | solution.py:25
  15.8 5.9 %collective-permute-start.3 = (bf16[1,3,22,256]{3,2,1,0:T(8,128)(2,1)S(1)}, bf16[1,3,22,256]{3,2,1,0:T(8,128)(2,1)S(1)}, u32[]{:S(2)}, u32[]{:S(2)}) collective-permute-start(bf16[1,3,22,256]{3,2,1,0:T(8,128)(2,1)S(1)} %get-tuple-element.77), channel_id=1, source_target_pairs={{1,0},{3,2},{5,4},{7,6},{9,8},{11,10},{13,12},{15,14},{17,16},{19,... | collective-permute-start | bytes 101384 | tf_op jit(solution)/shard_map/ppermute | solution.py:27
  19.2 13.9 %copy-start.4 = (f32[512,256]{1,0:T(8,128)}, f32[512,256]{1,0:T(8,128)S(1)}, u32[]{:S(2)}) copy-start(f32[512,256]{1,0:T(8,128)S(1)} %reshape.367) | copy-start | bytes 1572868
  109.4 14.9 %copy-start.10 = (f32[1,32,16,256]{3,2,1,0:T(8,128)S(1)}, f32[1,32,16,256]{3,2,1,0:T(8,128)}, u32[]{:S(2)}) copy-start(f32[1,32,16,256]{3,2,1,0:T(8,128)} %reshape.366) | copy-start | bytes 1572868
  109.4 14.9 %copy-start.22 = (f32[1,1,256]{2,1,0:T(1,128)S(1)}, f32[1,1,256]{2,1,0:T(1,128)}, u32[]{:S(2)}) copy-start(f32[1,1,256]{2,1,0:T(1,128)} %copy-done.21) | copy-start | bytes 3076
  109.4 15.0 %copy-start.24 = (f32[1,1,256]{2,1,0:T(1,128)S(1)}, f32[1,1,256]{2,1,0:T(1,128)}, u32[]{:S(2)}) copy-start(f32[1,1,256]{2,1,0:T(1,128)} %copy-done.23) | copy-start | bytes 3076
  109.4 15.0 %copy-start.26 = (f32[1,1,256]{2,1,0:T(1,128)S(1)}, f32[1,1,256]{2,1,0:T(1,128)}, u32[]{:S(2)}) copy-start(f32[1,1,256]{2,1,0:T(1,128)} %copy-done.25) | copy-start | bytes 3076
  109.4 15.0 %copy-start.28 = (f32[1,1,256]{2,1,0:T(1,128)S(1)}, f32[1,1,256]{2,1,0:T(1,128)}, u32[]{:S(2)}) copy-start(f32[1,1,256]{2,1,0:T(1,128)} %copy-done.27) | copy-start | bytes 3076
  109.4 15.0 %copy-start.30 = (f32[1,1,256]{2,1,0:T(1,128)S(1)}, f32[1,1,256]{2,1,0:T(1,128)}, u32[]{:S(2)}) copy-start(f32[1,1,256]{2,1,0:T(1,128)} %copy-done.29) | copy-start | bytes 3076
  109.4 15.0 %copy-start.32 = (f32[1,1,256]{2,1,0:T(1,128)S(1)}, f32[1,1,256]{2,1,0:T(1,128)}, u32[]{:S(2)}) copy-start(f32[1,1,256]{2,1,0:T(1,128)} %copy-done.31) | copy-start | bytes 3076
  109.4 15.0 %copy-start.34 = (f32[1,1,256]{2,1,0:T(1,128)S(1)}, f32[1,1,256]{2,1,0:T(1,128)}, u32[]{:S(2)}) copy-start(f32[1,1,256]{2,1,0:T(1,128)} %copy-done.33) | copy-start | bytes 3076
  109.4 15.0 %copy-start.36 = (f32[1,1,256]{2,1,0:T(1,128)S(1)}, f32[1,1,256]{2,1,0:T(1,128)}, u32[]{:S(2)}) copy-start(f32[1,1,256]{2,1,0:T(1,128)} %copy-done.35) | copy-start | bytes 3076
  109.4 15.0 %copy-start.38 = (f32[1,1,256]{2,1,0:T(1,128)S(1)}, f32[1,1,256]{2,1,0:T(1,128)}, u32[]{:S(2)}) copy-start(f32[1,1,256]{2,1,0:T(1,128)} %copy-done.37) | copy-start | bytes 3076
  109.5 15.0 %copy-start.40 = (f32[1,1,256]{2,1,0:T(1,128)S(1)}, f32[1,1,256]{2,1,0:T(1,128)}, u32[]{:S(2)}) copy-start(f32[1,1,256]{2,1,0:T(1,128)} %copy-done.39) | copy-start | bytes 3076
  109.5 15.0 %copy-start.42 = (f32[1,1,256]{2,1,0:T(1,128)S(1)}, f32[1,1,256]{2,1,0:T(1,128)}, u32[]{:S(2)}) copy-start(f32[1,1,256]{2,1,0:T(1,128)} %copy-done.41) | copy-start | bytes 3076
  109.5 15.0 %copy-start.44 = (f32[1,1,256]{2,1,0:T(1,128)S(1)}, f32[1,1,256]{2,1,0:T(1,128)}, u32[]{:S(2)}) copy-start(f32[1,1,256]{2,1,0:T(1,128)} %copy-done.43) | copy-start | bytes 3076
  109.5 15.0 %copy-start.46 = (f32[1,1,256]{2,1,0:T(1,128)S(1)}, f32[1,1,256]{2,1,0:T(1,128)}, u32[]{:S(2)}) copy-start(f32[1,1,256]{2,1,0:T(1,128)} %copy-done.45) | copy-start | bytes 3076
  109.5 15.0 %copy-start.48 = (f32[1,1,256]{2,1,0:T(1,128)S(1)}, f32[1,1,256]{2,1,0:T(1,128)}, u32[]{:S(2)}) copy-start(f32[1,1,256]{2,1,0:T(1,128)} %copy-done.47) | copy-start | bytes 3076
  109.5 15.0 %copy-start.50 = (f32[1,1,256]{2,1,0:T(1,128)S(1)}, f32[1,1,256]{2,1,0:T(1,128)}, u32[]{:S(2)}) copy-start(f32[1,1,256]{2,1,0:T(1,128)} %copy-done.49) | copy-start | bytes 3076
  109.5 15.0 %copy-start.52 = (f32[1,1,256]{2,1,0:T(1,128)S(1)}, f32[1,1,256]{2,1,0:T(1,128)}, u32[]{:S(2)}) copy-start(f32[1,1,256]{2,1,0:T(1,128)} %copy-done.51) | copy-start | bytes 3076
  109.5 15.0 %copy-start.54 = (f32[1,1,256]{2,1,0:T(1,128)S(1)}, f32[1,1,256]{2,1,0:T(1,128)}, u32[]{:S(2)}) copy-start(f32[1,1,256]{2,1,0:T(1,128)} %copy-done.53) | copy-start | bytes 3076
  109.5 15.0 %copy-start.56 = (f32[1,1,256]{2,1,0:T(1,128)S(1)}, f32[1,1,256]{2,1,0:T(1,128)}, u32[]{:S(2)}) copy-start(f32[1,1,256]{2,1,0:T(1,128)} %copy-done.55) | copy-start | bytes 3076
  109.5 15.0 %copy-start.58 = (f32[1,1,256]{2,1,0:T(1,128)S(1)}, f32[1,1,256]{2,1,0:T(1,128)}, u32[]{:S(2)}) copy-start(f32[1,1,256]{2,1,0:T(1,128)} %copy-done.57) | copy-start | bytes 3076
  109.6 15.0 %copy-start.60 = (f32[1,1,256]{2,1,0:T(1,128)S(1)}, f32[1,1,256]{2,1,0:T(1,128)}, u32[]{:S(2)}) copy-start(f32[1,1,256]{2,1,0:T(1,128)} %copy-done.59) | copy-start | bytes 3076
  109.6 15.0 %copy-start.62 = (f32[1,1,256]{2,1,0:T(1,128)S(1)}, f32[1,1,256]{2,1,0:T(1,128)}, u32[]{:S(2)}) copy-start(f32[1,1,256]{2,1,0:T(1,128)} %copy-done.61) | copy-start | bytes 3076
  109.6 15.0 %copy-start.64 = (f32[1,1,256]{2,1,0:T(1,128)S(1)}, f32[1,1,256]{2,1,0:T(1,128)}, u32[]{:S(2)}) copy-start(f32[1,1,256]{2,1,0:T(1,128)} %copy-done.63) | copy-start | bytes 3076
  109.6 15.0 %copy-start.66 = (f32[1,1,256]{2,1,0:T(1,128)S(1)}, f32[1,1,256]{2,1,0:T(1,128)}, u32[]{:S(2)}) copy-start(f32[1,1,256]{2,1,0:T(1,128)} %copy-done.65) | copy-start | bytes 3076
  109.6 15.0 %copy-start.68 = (f32[1,1,256]{2,1,0:T(1,128)S(1)}, f32[1,1,256]{2,1,0:T(1,128)}, u32[]{:S(2)}) copy-start(f32[1,1,256]{2,1,0:T(1,128)} %copy-done.67) | copy-start | bytes 3076
  109.6 15.0 %copy-start.70 = (f32[1,1,256]{2,1,0:T(1,128)S(1)}, f32[1,1,256]{2,1,0:T(1,128)}, u32[]{:S(2)}) copy-start(f32[1,1,256]{2,1,0:T(1,128)} %copy-done.69) | copy-start | bytes 3076
  109.6 15.0 %copy-start.72 = (f32[1,1,256]{2,1,0:T(1,128)S(1)}, f32[1,1,256]{2,1,0:T(1,128)}, u32[]{:S(2)}) copy-start(f32[1,1,256]{2,1,0:T(1,128)} %copy-done.71) | copy-start | bytes 3076
  109.6 15.0 %copy-start.74 = (f32[1,1,256]{2,1,0:T(1,128)S(1)}, f32[1,1,256]{2,1,0:T(1,128)}, u32[]{:S(2)}) copy-start(f32[1,1,256]{2,1,0:T(1,128)} %copy-done.73) | copy-start | bytes 3076
  109.6 15.0 %copy-start.76 = (f32[1,1,256]{2,1,0:T(1,128)S(1)}, f32[1,1,256]{2,1,0:T(1,128)}, u32[]{:S(2)}) copy-start(f32[1,1,256]{2,1,0:T(1,128)} %copy-done.75) | copy-start | bytes 3076
  109.6 15.0 %copy-start.78 = (f32[1,1,256]{2,1,0:T(1,128)S(1)}, f32[1,1,256]{2,1,0:T(1,128)}, u32[]{:S(2)}) copy-start(f32[1,1,256]{2,1,0:T(1,128)} %copy-done.77) | copy-start | bytes 3076
  109.7 15.0 %copy-start.80 = (f32[1,1,256]{2,1,0:T(1,128)S(1)}, f32[1,1,256]{2,1,0:T(1,128)}, u32[]{:S(2)}) copy-start(f32[1,1,256]{2,1,0:T(1,128)} %copy-done.79) | copy-start | bytes 3076
  109.7 15.0 %copy-start.82 = (f32[1,1,256]{2,1,0:T(1,128)S(1)}, f32[1,1,256]{2,1,0:T(1,128)}, u32[]{:S(2)}) copy-start(f32[1,1,256]{2,1,0:T(1,128)} %copy-done.81) | copy-start | bytes 3076
  109.7 15.0 %copy-start.84 = (f32[1,1,256]{2,1,0:T(1,128)S(1)}, f32[1,1,256]{2,1,0:T(1,128)}, u32[]{:S(2)}) copy-start(f32[1,1,256]{2,1,0:T(1,128)} %copy-done.83) | copy-start | bytes 3076
  109.7 15.0 %copy-start.86 = (f32[1,1,256]{2,1,0:T(1,128)S(1)}, f32[1,1,256]{2,1,0:T(1,128)}, u32[]{:S(2)}) copy-start(f32[1,1,256]{2,1,0:T(1,128)} %copy-done.85) | copy-start | bytes 3076
  109.7 15.0 %copy-start.88 = (f32[1,1,256]{2,1,0:T(1,128)S(1)}, f32[1,1,256]{2,1,0:T(1,128)}, u32[]{:S(2)}) copy-start(f32[1,1,256]{2,1,0:T(1,128)} %copy-done.87) | copy-start | bytes 3076
  109.7 15.0 %copy-start.90 = (f32[1,1,256]{2,1,0:T(1,128)S(1)}, f32[1,1,256]{2,1,0:T(1,128)}, u32[]{:S(2)}) copy-start(f32[1,1,256]{2,1,0:T(1,128)} %copy-done.89) | copy-start | bytes 3076
  109.7 15.0 %copy-start.92 = (f32[1,1,256]{2,1,0:T(1,128)S(1)}, f32[1,1,256]{2,1,0:T(1,128)}, u32[]{:S(2)}) copy-start(f32[1,1,256]{2,1,0:T(1,128)} %copy-done.91) | copy-start | bytes 3076
  109.7 6.4 %collective-permute-start.4 = (bf16[1,32,3,256]{3,2,1,0:T(4,128)(2,1)S(1)}, bf16[1,32,3,256]{3,2,1,0:T(4,128)(2,1)S(1)}, u32[]{:S(2)}, u32[]{:S(2)}) collective-permute-start(bf16[1,32,3,256]{3,2,1,0:T(4,128)(2,1)S(1)} %copy-done.19), channel_id=1, source_target_pairs={{0,2},{2,4},{4,6},{6,8},{8,10},{10,12},{12,14},{14,16},{16,18},{18... | collective-permute-start | bytes 147464 | tf_op jit(solution)/shard_map/ppermute | solution.py:25
  110.2 14.5 %copy-start.94 = (f32[1,1,256]{2,1,0:T(1,128)S(1)}, f32[1,1,256]{2,1,0:T(1,128)}, u32[]{:S(2)}) copy-start(f32[1,1,256]{2,1,0:T(1,128)} %copy-done.93) | copy-start | bytes 3076
  110.2 6.0 %collective-permute-start.5 = (bf16[1,32,3,256]{3,2,1,0:T(4,128)(2,1)S(1)}, bf16[1,32,3,256]{3,2,1,0:T(4,128)(2,1)S(1)}, u32[]{:S(2)}, u32[]{:S(2)}) collective-permute-start(bf16[1,32,3,256]{3,2,1,0:T(4,128)(2,1)S(1)} %copy-done.18), channel_id=1, source_target_pairs={{2,0},{4,2},{6,4},{8,6},{10,8},{12,10},{14,12},{16,14},{18,16},{20... | collective-permute-start | bytes 147464 | tf_op jit(solution)/shard_map/ppermute | solution.py:27
  116.2 5.0 %collective-permute-start.6 = (bf16[1,3,22,256]{3,2,1,0:T(8,128)(2,1)S(1)}, bf16[1,3,22,256]{3,2,1,0:T(8,128)(2,1)S(1)}, u32[]{:S(2)}, u32[]{:S(2)}) collective-permute-start(bf16[1,3,22,256]{3,2,1,0:T(8,128)(2,1)S(1)} %get-tuple-element.74), channel_id=1, source_target_pairs={{0,1},{2,3},{4,5},{6,7},{8,9},{10,11},{12,13},{14,15},{16,17},{18,... | collective-permute-start | bytes 101384 | tf_op jit(solution)/shard_map/ppermute | solution.py:25
  118.3 5.9 %collective-permute-start.7 = (bf16[1,3,22,256]{3,2,1,0:T(8,128)(2,1)S(1)}, bf16[1,3,22,256]{3,2,1,0:T(8,128)(2,1)S(1)}, u32[]{:S(2)}, u32[]{:S(2)}) collective-permute-start(bf16[1,3,22,256]{3,2,1,0:T(8,128)(2,1)S(1)} %get-tuple-element.75), channel_id=1, source_target_pairs={{1,0},{3,2},{5,4},{7,6},{9,8},{11,10},{13,12},{15,14},{17,16},{19,... | collective-permute-start | bytes 101384 | tf_op jit(solution)/shard_map/ppermute | solution.py:27
  (64 other events, 572.3 us)

commit v2 on v1

v2 whole, which is shorter than its diff:
```python
from functools import partial
import math

import jax
import jax.numpy as jnp
from jax import lax
from jax.experimental import pallas as pl
from jax.experimental.pallas import tpu as pltpu
from jax.sharding import PartitionSpec as P

PARAMS = 1061632


EPS = 1e-06


MESH = pl.DeviceIdType.MESH


def exchange_copies(edges, cells, side, ends, corner, ssem, rsem, sizes):
    lon, lat = lax.axis_index("lon"), lax.axis_index("lat")
    nlon, _ = sizes
    rows = cells.shape[0]
    left = lax.rem(lon + nlon - 1, nlon)
    right = lax.rem(lon + 1, nlon)

    def copy(src, dst, n, where):
        return pltpu.make_async_remote_copy(
            src_ref=src,
            dst_ref=dst,
            send_sem=ssem.at[n],
            recv_sem=rsem.at[n],
            device_id=where,
            device_id_type=MESH,
        )

    across = [
        copy(edges.at[0:3], side.at[1], 0, {"lon": left, "lat": lat}),
        copy(edges.at[3:6], side.at[0], 1, {"lon": right, "lat": lat}),
    ]
    above = lat - 1
    below = lat + 1
    up = [
        copy(cells.at[0:3], ends.at[1], 2, {"lon": lon, "lat": above}),
        copy(edges.at[0:3, 0:16], corner.at[1, 1], 3, {"lon": left, "lat": above}),
        copy(edges.at[3:6, 0:16], corner.at[1, 0], 4, {"lon": right, "lat": above}),
    ]
    down = [
        copy(cells.at[rows - 3 : rows], ends.at[0], 5, {"lon": lon, "lat": below}),
        copy(edges.at[0:3, rows - 16 : rows], corner.at[0, 1], 6, {"lon": left, "lat": below}),
        copy(edges.at[3:6, rows - 16 : rows], corner.at[0, 0], 7, {"lon": right, "lat": below}),
    ]
    return across, up, down


def greet(barrier, sizes):
    lon, lat = lax.axis_index("lon"), lax.axis_index("lat")
    nlon, nlat = sizes
    left = lax.rem(lon + nlon - 1, nlon)
    right = lax.rem(lon + 1, nlon)

    def signal(where):
        pl.semaphore_signal(barrier, inc=1, device_id=where, device_id_type=MESH)

    signal({"lon": left, "lat": lat})
    signal({"lon": right, "lat": lat})
    for there, ok in ((lat - 1, lat > 0), (lat + 1, lat < nlat - 1)):

        @pl.when(ok)
        def _():
            for other in (left, lon, right):
                signal({"lon": other, "lat": there})


def await_greetings(barrier, sizes, extra):
    lat = lax.axis_index("lat")
    beside = jnp.minimum(lat, 1) + jnp.minimum(sizes[1] - 1 - lat, 1)
    pl.semaphore_wait(barrier, 2 + extra + 3 * beside)


def exchange_start(edges, cells, side, ends, corner, ssem, rsem, sizes):
    lat = lax.axis_index("lat")
    across, up, down = exchange_copies(edges, cells, side, ends, corner, ssem, rsem, sizes)
    for c in across:
        c.start()

    @pl.when(lat > 0)
    def _():
        for c in up:
            c.start()

    @pl.when(lat < sizes[1] - 1)
    def _():
        for c in down:
            c.start()


def exchange_finish(edges, cells, side, ends, corner, ssem, rsem, sizes):
    lat = lax.axis_index("lat")
    across, up, down = exchange_copies(edges, cells, side, ends, corner, ssem, rsem, sizes)
    for c in across:
        c.wait()

    @pl.when(lat > 0)
    def _():
        for sent, came in zip(up, down):
            sent.wait_send()
            came.wait_recv()

    @pl.when(lat < sizes[1] - 1)
    def _():
        for sent, came in zip(down, up):
            sent.wait_send()
            came.wait_recv()

    @pl.when(lat == 0)
    def _():
        ends[0] = jnp.zeros(ends.shape[1:], ends.dtype)
        corner[0] = jnp.zeros(corner.shape[1:], corner.dtype)

    @pl.when(lat == sizes[1] - 1)
    def _():
        ends[1] = jnp.zeros(ends.shape[1:], ends.dtype)
        corner[1] = jnp.zeros(corner.shape[1:], corner.dtype)


def halo_body(sizes, edges, cells, side, ends, corner, ssem, rsem):
    barrier = pltpu.get_barrier_semaphore()
    greet(barrier, sizes)
    await_greetings(barrier, sizes, 0)
    exchange_start(edges, cells, side, ends, corner, ssem, rsem, sizes)
    exchange_finish(edges, cells, side, ends, corner, ssem, rsem, sizes)


def halo_shapes(cells):
    rows, cols, channels = cells.shape
    return [
        jax.ShapeDtypeStruct((2, 3, rows, channels), jnp.bfloat16),
        jax.ShapeDtypeStruct((2, 3, cols, channels), jnp.bfloat16),
        jax.ShapeDtypeStruct((2, 2, 3, 16, channels), jnp.bfloat16),
    ]


HALVES = (slice(0, 128), slice(128, 256))
VMEM_SPEC = pl.BlockSpec(memory_space=pltpu.VMEM)


def halo(edges, cells, mesh_shape):
    return pl.pallas_call(
        partial(halo_body, (mesh_shape["lon"], mesh_shape["lat"])),
        name="field_halo",
        out_shape=halo_shapes(cells),
        in_specs=[VMEM_SPEC] * 2,
        out_specs=[VMEM_SPEC] * 3,
        scratch_shapes=[pltpu.SemaphoreType.DMA((8,)), pltpu.SemaphoreType.DMA((8,))],
        compiler_params=pltpu.CompilerParams(
            collective_id=0, has_side_effects=True, vmem_limit_bytes=8 << 20
        ),
    )(edges, cells)


def extend(cells, side, ends, corner, wide, shifted):
    rows, cols, _ = cells.shape
    f32 = jnp.float32

    def put(where, values):
        values = values.astype(f32)
        for h in range(2):
            wide[h, where, :] = values[:, HALVES[h]]

    def fill(r, carry):
        put(pl.ds(pl.multiple_of((3 + r) * 32 + 8, 8), cols), cells[r])
        return carry

    lax.fori_loop(0, rows, fill, 0)
    for r in range(3):
        put(pl.ds(r * 32 + 8, cols), ends[0, r])
        put(pl.ds((rows + 3 + r) * 32 + 8, cols), ends[1, r])
    for h in range(2):
        for s, first in ((0, 5), (1, 8 + cols)):
            for c in range(3):
                column = first + c
                wide[h, pl.ds(3 * 32 + column, rows, stride=32), :] = side[
                    s, c, :, HALVES[h]
                ].astype(f32)
    for s, first in ((0, 5), (1, 8 + cols)):
        for c in range(3):
            high = corner[0, s, c].astype(f32)
            low = corner[1, s, c].astype(f32)
            for r in range(3):
                put(pl.ds(r * 32 + first + c, 1), high[13 + r : 14 + r])
                put(pl.ds((rows + 3 + r) * 32 + first + c, 1), low[r : r + 1])

    def shift(r, carry):
        for h in range(2):
            v = wide[h, pl.ds(pl.multiple_of(r * 32, 32), 32), :]
            for q in range(7):
                shifted[q, r, :, HALVES[h]] = pltpu.roll(v, 27 - q, 0)[:cols]
        return carry

    lax.fori_loop(0, rows + 6, shift, 0)


def spread_rows(shifted, kernel, first, count, flip):
    total = None
    for q in range(7):
        for p in range(7):
            at = (6 - p) * 7 + (6 - q) if flip else p * 7 + q
            term = shifted[q, pl.ds(first + p, count)] * kernel[at : at + 1, :]
            total = term if total is None else total + term
    return total


def dot(a, b, contract):
    return lax.dot_general(a, b, ((contract[0:1], contract[1:2]), ((), ())), preferred_element_type=jnp.float32)


def block_body(
    cells, side, ends, corner, kernel, gain, inner, outer, scale, down, cotangent,
    coarse, grad_cells, grad_depth, grad_edges, raw_inner, raw_outer, raw_down, small,
    wide, shifted, mixed, grad_wide, blocked, normed, hidden, grad_pre, grad_branch, terms,
):
    rows, cols, channels = cells.shape
    f32, bf16 = jnp.float32, jnp.bfloat16
    cot = cotangent[...]
    pair = cols // 2
    for p in range(2):
        for q in range(2):
            at = (2 * p + q) * channels
            gp = dot(cot, down[at : at + channels, :], (1, 1)).astype(bf16).astype(f32)
            for i in range(rows // 2):
                first = (2 * i + p) * cols + q
                for lane in range(2):
                    grad_wide[lane, pl.ds(first, pair, stride=2), :] = gp[i * pair : (i + 1) * pair, HALVES[lane]]

    extend(cells, side, ends, corner, wide, shifted)

    def convolve(t, carry):
        first = t * 8
        out = spread_rows(shifted, kernel, first, 8, False)
        mixed[pl.ds(pl.multiple_of(first * cols, 128), 8 * cols), :] = out.reshape(8 * cols, channels)
        return carry

    lax.fori_loop(0, rows // 8, convolve, 0)

    small[...] = jnp.zeros(small.shape, f32)
    chunk = 16 * cols
    g = gain[...]
    ls = scale[...]

    def step(t, carry):
        raw_gain, raw_scale = carry
        here = pl.ds(pl.multiple_of(t * chunk, chunk), chunk)
        m = mixed[here, :]
        centered = m - jnp.mean(m, axis=-1, keepdims=True)
        inv = lax.rsqrt(jnp.mean(centered * centered, axis=-1, keepdims=True) + EPS)
        xhat = centered * inv
        nrm = (xhat * g).astype(bf16)
        normed[here, :] = nrm
        pre = dot(nrm, inner[...], (1, 0))
        cdf = 0.5 * (1.0 + lax.erf(pre * math.sqrt(0.5)))
        slope = cdf + pre * (jnp.exp(-0.5 * pre * pre) * (1.0 / math.sqrt(2.0 * math.pi)))
        hid = (pre * cdf).astype(bf16)
        hidden[here, :] = hid
        branch = dot(hid, outer[...], (1, 0))
        field = cells[pl.ds(t * 16, 16)].astype(f32).reshape(chunk, channels)
        block_out = (field + ls * branch).astype(bf16).astype(f32)
        for h in range(2):
            blocked[h, here, :] = block_out[:, HALVES[h]]
        gb = jnp.concatenate([grad_wide[h, here, :] for h in range(2)], axis=1)
        grad_cells[here, :] = gb.astype(bf16)
        raw_scale = raw_scale + jnp.sum(gb * branch, axis=0, keepdims=True)
        gbr = (gb * ls).astype(bf16)
        grad_branch[here, :] = gbr
        gp = (dot(gbr, outer[...], (1, 1)) * slope).astype(bf16)
        grad_pre[here, :] = gp
        gn = dot(gp, inner[...], (1, 1))
        raw_gain = raw_gain + jnp.sum(gn * xhat, axis=0, keepdims=True)
        gx = gn * g
        m1 = jnp.mean(gx, axis=-1, keepdims=True)
        m2 = jnp.mean(gx * xhat, axis=-1, keepdims=True)
        gd = ((gx - m1 - xhat * m2) * inv).astype(bf16)
        grad_depth[pl.ds(t * 16, 16)] = gd.reshape(16, cols, channels)
        gd = gd.astype(f32)
        mixed[here, :] = gd
        for h in range(2):
            grad_wide[h, here, :] = gd[:, HALVES[h]]
        return raw_gain, raw_scale

    zero = jnp.zeros((1, channels), f32)
    raw_gain, raw_scale = lax.fori_loop(0, rows // 16, step, (zero, zero))
    small[49:50, :] = raw_gain
    small[50:51, :] = raw_scale
    raw_outer[...] = dot(hidden[...], grad_branch[...], (0, 0))
    raw_inner[...] = dot(normed[...], grad_pre[...], (0, 0))
    total = None
    for p in range(2):
        for q in range(2):
            at = (2 * p + q) * channels
            lanes = []
            for h in range(2):
                lanes.append(
                    jnp.concatenate(
                        [
                            blocked[h, pl.ds((2 * i + p) * cols + q, pair, stride=2), :]
                            for i in range(rows // 2)
                        ]
                    ).astype(bf16)
                )
            patch = jnp.concatenate(lanes, axis=1)
            part = dot(patch, down[at : at + channels, :], (1, 0))
            total = part if total is None else total + part
            raw_down[at : at + channels, :] = dot(patch, cot, (0, 0))
    coarse[...] = total.astype(bf16)

    terms[...] = jnp.zeros(terms.shape, f32)

    def kernel_step(t, carry):
        first = t * 4
        gd = mixed[pl.ds(pl.multiple_of(first * cols, 64), 4 * cols), :].reshape(4, cols, channels)
        for q in range(7):
            for p in range(7):
                prod = shifted[q, pl.ds(first + p, 4)] * gd
                prod = (prod[0] + prod[1]) + (prod[2] + prod[3])
                terms[p * 7 + q] = terms[p * 7 + q] + (prod[0:8] + prod[8:16])
        return carry

    lax.fori_loop(0, rows // 4, kernel_step, 0)
    small[0:49, :] = jnp.sum(terms[...], axis=1)
    for h in range(2):
        for c in range(3):
            for at, column in ((c, c), (3 + c, cols - 3 + c)):
                grad_edges[at, :, HALVES[h]] = grad_wide[
                    h, pl.ds(column, rows, stride=cols), :
                ].astype(bf16)


def block(cells, halos, kernel, gain, inner, outer, scale, down, cotangent):
    rows, cols, channels = cells.shape
    count = rows * cols
    hid = inner.shape[1]
    f32, bf16 = jnp.float32, jnp.bfloat16
    return pl.pallas_call(
        block_body,
        name="block",
        out_shape=[
            jax.ShapeDtypeStruct(cotangent.shape, bf16),
            jax.ShapeDtypeStruct((count, channels), bf16),
            jax.ShapeDtypeStruct(cells.shape, bf16),
            jax.ShapeDtypeStruct((6, rows, channels), bf16),
            jax.ShapeDtypeStruct(inner.shape, f32),
            jax.ShapeDtypeStruct(outer.shape, f32),
            jax.ShapeDtypeStruct(down.shape, f32),
            jax.ShapeDtypeStruct((64, channels), f32),
        ],
        in_specs=[VMEM_SPEC] * 11,
        out_specs=[VMEM_SPEC] * 8,
        scratch_shapes=[
            pltpu.VMEM((2, (rows + 6) * 32, channels // 2), f32),
            pltpu.VMEM((7, rows + 6, cols, channels), f32),
            pltpu.VMEM((count, channels), f32),
            pltpu.VMEM((2, count, channels // 2), f32),
            pltpu.VMEM((2, count, channels // 2), f32),
            pltpu.VMEM((count, channels), bf16),
            pltpu.VMEM((count, hid), bf16),
            pltpu.VMEM((count, hid), bf16),
            pltpu.VMEM((count, channels), bf16),
            pltpu.VMEM((49, 8, channels), f32),
        ],
        compiler_params=pltpu.CompilerParams(vmem_limit_bytes=48 << 20),
    )(cells, *halos, kernel, gain, inner, outer, scale, down, cotangent)


def place(mesh_shape):
    lon_bits = mesh_shape["lon"].bit_length() - 1
    lat_bits = mesh_shape["lat"].bit_length() - 1
    core = ("lon", 0)
    groups = [
        [("lat", k) for k in range(lat_bits)],
        [("lon", k) for k in range(1, min(2, lon_bits))],
        [("lon", k) for k in range(2, lon_bits)],
    ]
    orders = []
    for p in range(3):
        rotated = groups[p:] + groups[:p]
        orders.append([core] + [bit for group in rotated for bit in group])
    devices = mesh_shape["lon"] * mesh_shape["lat"]
    unit = 3 * 16 * devices
    rows = -(-(4096 + 64) // unit) * unit
    return orders, rows, devices


def partner_of(bit):
    axis, k = bit
    me = lax.axis_index(axis)
    b = lax.rem(lax.div(me, 2**k), 2)
    return b, {axis: me + (1 - 2 * b) * 2**k}


def sum_kernel_body(
    orders, devices, sizes, edges, cells, inner, outer, down, small,
    out, side, ends, corner, acc, send, recv, ssem, rsem, halo_ssem, halo_rsem,
):
    rows = acc.shape[0]
    part_rows = rows // 3
    stages = len(orders[0])
    barrier = pltpu.get_barrier_semaphore()
    for bit in orders[0]:
        _, device = partner_of(bit)
        pl.semaphore_signal(barrier, inc=1, device_id=device, device_id_type=MESH)
    greet(barrier, sizes)

    def pack_inner(i, carry):
        r = pl.multiple_of(i * 64, 64)
        for c in range(4):
            acc[pl.ds(c * 256 + r, 64), :] = inner[pl.ds(r, 64), c * 256 : (c + 1) * 256]
        return carry

    lax.fori_loop(0, 4, pack_inner, 0)

    def pack_rest(i, carry):
        r = pl.multiple_of(i * 64, 64)
        acc[pl.ds(1024 + r, 64), :] = outer[pl.ds(r, 64), :]
        acc[pl.ds(2048 + r, 64), :] = down[pl.ds(r, 64), 0:256]
        acc[pl.ds(3072 + r, 64), :] = down[pl.ds(r, 64), 256:512]
        return carry

    lax.fori_loop(0, 16, pack_rest, 0)
    acc[4096:4160, :] = small[...]

    def clear(i, carry):
        acc[pl.ds(pl.multiple_of(4160 + i * 32, 32), 32), :] = jnp.zeros((32, 256), jnp.float32)
        return carry

    lax.fori_loop(0, (rows - 4160) // 32, clear, 0)
    await_greetings(barrier, sizes, stages)
    exchange_start(edges, cells, side, ends, corner, halo_ssem, halo_rsem, sizes)

    unit = part_rows // devices
    offs = [p * part_rows for p in range(3)]
    keeps = [[None] * stages for _ in range(3)]
    sent = []

    def start(s, p):
        b, device = partner_of(orders[p][s])
        half = part_rows >> (s + 1)
        base = p * part_rows + part_rows - 2 * half
        away = offs[p] + (1 - b) * half
        keeps[p][s] = offs[p] + b * half
        chunk = min(half, 4 * unit)

        def cast(i, carry):
            r = i * chunk
            send[pl.ds(pl.multiple_of(base + r, 16), chunk), :] = acc[
                pl.ds(pl.multiple_of(away + r, 16), chunk), :
            ].astype(jnp.bfloat16)
            return carry

        lax.fori_loop(0, half // chunk, cast, 0)
        copy = pltpu.make_async_remote_copy(
            src_ref=send.at[pl.ds(base, half)],
            dst_ref=recv.at[pl.ds(base, half)],
            send_sem=ssem.at[p, s],
            recv_sem=rsem.at[p, s],
            device_id=device,
            device_id_type=MESH,
        )
        copy.start()
        sent.append(copy)
        return copy

    def finish(s, p, copy):
        half = part_rows >> (s + 1)
        base = p * part_rows + part_rows - 2 * half
        keep = keeps[p][s]
        chunk = min(half, 4 * unit)
        copy.wait_recv()

        def add(i, carry):
            r = i * chunk
            mine = pl.ds(pl.multiple_of(keep + r, 16), chunk)
            acc[mine, :] = acc[mine, :] + recv[
                pl.ds(pl.multiple_of(base + r, 16), chunk), :
            ].astype(jnp.float32)
            return carry

        lax.fori_loop(0, half // chunk, add, 0)
        offs[p] = keep

    def spread(s, p):
        _, device = partner_of(orders[p][s])
        half = part_rows >> (s + 1)
        mine = pl.ds(pl.multiple_of(keeps[p][s], 16), half)
        copy = pltpu.make_async_remote_copy(
            src_ref=out.at[mine],
            dst_ref=out.at[mine],
            send_sem=ssem.at[p, stages + s],
            recv_sem=rsem.at[p, stages + s],
            device_id=device,
            device_id_type=MESH,
        )
        copy.start()
        sent.append(copy)
        return copy

    flight = [start(0, p) for p in range(3)]
    for s in range(stages):
        for p in range(3):
            finish(s, p, flight[p])
            if s + 1 < stages:
                flight[p] = start(s + 1, p)
            else:
                mine = pl.ds(pl.multiple_of(offs[p], 16), unit)
                out[mine, :] = acc[mine, :].astype(jnp.bfloat16)
                flight[p] = spread(stages - 1, p)
    for s in range(stages - 2, -1, -1):
        for p in range(3):
            flight[p].wait_recv()
            flight[p] = spread(s, p)
    for p in range(3):
        flight[p].wait_recv()
    for copy in sent:
        copy.wait_send()
    exchange_finish(edges, cells, side, ends, corner, halo_ssem, halo_rsem, sizes)


def summed(edges, cells, inner, outer, down, small, mesh_shape):
    orders, rows, devices = place(mesh_shape)
    stages = len(orders[0])
    return pl.pallas_call(
        partial(sum_kernel_body, orders, devices, (mesh_shape["lon"], mesh_shape["lat"])),
        name="sum_gradients",
        out_shape=[jax.ShapeDtypeStruct((rows, 256), jnp.bfloat16)] + halo_shapes(cells),
        in_specs=[VMEM_SPEC] * 6,
        out_specs=[VMEM_SPEC] * 4,
        scratch_shapes=[
            pltpu.VMEM((rows, 256), jnp.float32),
            pltpu.VMEM((rows, 256), jnp.bfloat16),
            pltpu.VMEM((rows, 256), jnp.bfloat16),
            pltpu.SemaphoreType.DMA((3, 2 * stages)),
            pltpu.SemaphoreType.DMA((3, 2 * stages)),
            pltpu.SemaphoreType.DMA((8,)),
            pltpu.SemaphoreType.DMA((8,)),
        ],
        compiler_params=pltpu.CompilerParams(
            collective_id=1, has_side_effects=True, vmem_limit_bytes=48 << 20
        ),
    )(edges, cells, inner, outer, down, small)


def finish_body(
    sums, cells, side, ends, corner, kernel, grad_cells,
    inner, outer, down, small, grad_field, wide, shifted,
):
    def squares(i, total):
        v = sums[pl.ds(pl.multiple_of(i * 64, 64), 64), :].astype(jnp.float32)
        v = v * v
        for width in (32, 16, 8):
            v = v[:width] + v[width:]
        return total + v

    total = jnp.sum(lax.fori_loop(0, 65, squares, jnp.zeros((8, 256), jnp.float32)))
    total = jnp.full((1, 256), total, jnp.float32)
    factor = jnp.minimum(1.0, math.sqrt(PARAMS) / jnp.sqrt(total + EPS))

    def write_inner(i, carry):
        r = pl.multiple_of(i * 64, 64)
        for c in range(4):
            inner[pl.ds(r, 64), c * 256 : (c + 1) * 256] = (
                sums[pl.ds(c * 256 + r, 64), :].astype(jnp.float32) * factor
            )
        return carry

    lax.fori_loop(0, 4, write_inner, 0)

    def write_rest(i, carry):
        r = pl.multiple_of(i * 64, 64)
        outer[pl.ds(r, 64), :] = sums[pl.ds(1024 + r, 64), :].astype(jnp.float32) * factor
        down[pl.ds(r, 64), 0:256] = sums[pl.ds(2048 + r, 64), :].astype(jnp.float32) * factor
        down[pl.ds(r, 64), 256:512] = sums[pl.ds(3072 + r, 64), :].astype(jnp.float32) * factor
        return carry

    lax.fori_loop(0, 16, write_rest, 0)
    small[...] = sums[4096:4160, :].astype(jnp.float32) * factor
    rows, cols, channels = cells.shape
    extend(cells, side, ends, corner, wide, shifted)

    def convolve(t, carry):
        first = t * 8
        here = pl.ds(pl.multiple_of(first * cols, 128), 8 * cols)
        out = spread_rows(shifted, kernel, first, 8, True).reshape(8 * cols, channels)
        grad_field[here, :] = (grad_cells[here, :].astype(jnp.float32) + out).astype(jnp.bfloat16)
        return carry

    lax.fori_loop(0, rows // 8, convolve, 0)


def finished(sums, cells, halos, kernel, grad_cells):
    rows, cols, channels = cells.shape
    f32 = jnp.float32
    shapes = ((256, 1024), (1024, 256), (1024, 512), (64, 256))
    return pl.pallas_call(
        finish_body,
        name="finish",
        out_shape=[jax.ShapeDtypeStruct(shape, f32) for shape in shapes]
        + [jax.ShapeDtypeStruct(grad_cells.shape, jnp.bfloat16)],
        in_specs=[VMEM_SPEC] * 7,
        out_specs=[VMEM_SPEC] * 5,
        scratch_shapes=[
            pltpu.VMEM((2, (rows + 6) * 32, channels // 2), f32),
            pltpu.VMEM((7, rows + 6, cols, channels), f32),
        ],
        compiler_params=pltpu.CompilerParams(vmem_limit_bytes=48 << 20),
    )(sums, cells, *halos, kernel, grad_cells)


def body(
    mesh_shape,
    field,
    depth_kernel,
    layer_norm_gain,
    inner_weight,
    outer_weight,
    layer_scale,
    down_weight,
    cotangent,
):
    _, rows, cols, channels = field.shape
    cells = field[0]
    edges = jnp.concatenate([cells[:, :3], cells[:, cols - 3 :]], axis=1).transpose(1, 0, 2)
    kernel = depth_kernel.reshape(49, channels)
    halos = halo(edges, cells, mesh_shape)
    coarse, grad_cells, grad_depth, grad_edges, raw_inner, raw_outer, raw_down, small = block(
        cells,
        halos,
        kernel,
        layer_norm_gain[None],
        inner_weight,
        outer_weight,
        layer_scale[None],
        down_weight,
        cotangent.reshape(-1, cotangent.shape[3]),
    )
    sums, *grad_halos = summed(
        grad_edges, grad_depth, raw_inner, raw_outer, raw_down, small, mesh_shape
    )
    grad_inner, grad_outer, grad_down, grad_small, grad_field = finished(
        sums, grad_depth, grad_halos, kernel, grad_cells
    )
    return (
        coarse.reshape(cotangent.shape),
        grad_field.reshape(field.shape),
        grad_small[:49].reshape(7, 7, channels),
        grad_small[49],
        grad_inner,
        grad_outer,
        grad_small[50],
        grad_down,
    )


def solution(mesh):
    return jax.shard_map(
        partial(body, dict(mesh.shape)),
        mesh=mesh,
        in_specs=(
            P(None, "lat", "lon", None),
            P(),
            P(),
            P(),
            P(),
            P(),
            P(),
            P(None, "lat", "lon", None),
        ),
        out_specs=(
            P(None, "lat", "lon", None),
            P(None, "lat", "lon", None),
            P(),
            P(),
            P(),
            P(),
            P(),
            P(),
        ),
        check_vma=False,
    )
```

time: 131 us -> 86.1 us (0.66)
  Pallas kernels: 48.5 us -> 71.1 us
  other arithmetic: 18.8 us -> 0.07 us
  starting transfers between devices: 18.5 us -> 0 us
  matrix products: 14.9 us -> 0 us
  local copies, waits for them, and re-layouts: 21.3 us -> 13.8 us
  waiting for transfers between devices: 5.57 us -> 0 us
  between operations: 2.21 us -> 0.7 us
    pallas_call x2 -> x4, Pallas kernels: 48.5 us -> 71.1 us  [the longest x1 45.5 us: summed(): pl.pallas_call(partial(sum_kernel_body, orders, devices, (mesh_shape['lon...]
    ppermute x8 -> x0, starting transfers between devices: 18.5 us -> none  [the longest x4 11.7 us: padded_2(): lax.ppermute(head, axis, [((i + 1) % count, i) for i in range(ends)])]
    dot_general x9 -> x0, matrix products: 14.9 us -> none  [the longest x1 5.62 us: body(): jnp.dot(normalized_output, inner_weight, preferred_element_type=jnp.float32)]
    reduce_sum x6 -> x0, other arithmetic: 11.7 us -> none  [the longest x3 5.97 us: kernel_terms(): jnp.sum(padded[:, row_shift:row_shift + rows, col_shift:col_shift + cols]...]
    convert_element_type x4 -> x0, other arithmetic: 5.65 us -> none  [the longest x1 5.08 us: body(): (grad_blocked.reshape(field.shape).astype(jnp.float32) + spread).astype(j...]
    ppermute x8 -> x0, waiting for transfers between devices: 5.57 us -> none  [the longest x4 4.2 us: padded_2(): lax.ppermute(head, axis, [((i + 1) % count, i) for i in range(ends)])]
    concatenate x1 -> x0, local copies, waits for them, and re-layouts: 5.14 us -> none  [body(): jnp.concatenate([raw_kernel.reshape(49, channel_count), unclipped_gain[No...]
    unnamed x208 -> x20, local copies, waits for them, and re-layouts: 5.99 us -> 10.7 us
  transfers between devices with their start and end apart: 8 -> 0, of which waited for: 3 -> 0; matrix products, arithmetic and copies ran while one was open for 7% -> 0% of each run, Pallas kernels for 0% -> 0%
where the time goes in v2:
time: 86.1 us; the launch traced here: 85.6 us
  Pallas kernels  71.1 us (83%)
  local copies, waits for them, and re-layouts  13.8 us (16%)
    pallas_call x1, Pallas kernels, summed(): pl.pallas_call(partial(sum_kernel_body, orders, devices, (mesh_shape['lon...  45.5 us
    unnamed x20, local copies, waits for them, and re-layouts  10.7 us
    pallas_call x1, Pallas kernels, block(): pl.pallas_call(block_body, name='block', out_shape=[jax.ShapeDtypeStruct(...  9.86 us
    pallas_call x1, Pallas kernels, halo(): pl.pallas_call(partial(halo_body, (mesh_shape['lon'], mesh_shape['lat']))...  9.43 us
    pallas_call x1, Pallas kernels, finished(): pl.pallas_call(finish_body, name='finish', out_shape=[jax.ShapeDtypeStruc...  6.25 us

profile of v2, /device:TPU:0, one launch (start us, length us, event | category | flops | bytes accessed | tf_op | source)
XLA Modules:
  0.0 85.6 jit_solution(244787942574751827)
XLA Ops:
  0.6 0.8 reshape.31.kernel
  1.5 1.0 %fusion = (bf16[32,3,256]{2,1,0:T(4,128)(2,1)S(1)}, bf16[32,3,256]{2,1,0:T(4,128)(2,1)S(1)}) fusion(bf16[32,16,256]{2,1,0:T(8,128)(2,1)} %bitcast.10), kind=kLoop, calls=%fused_computation.1 | loop fusion | bytes 196608 | tf_op jit(solution)/shard_map/slice | solution.py:630
  2.5 0.1 maximum_bitcast_fusion
  2.6 0.0 copy-start.2
  2.6 0.9 %copy-done.2 = bf16[1,32,16,256]{3,2,1,0:T(8,128)(2,1)S(1)} copy-done((bf16[1,32,16,256]{3,2,1,0:T(8,128)(2,1)S(1)}, bf16[1,32,16,256]{3,2,1,0:T(8,128)(2,1)}, u32[]{:S(2)}) %copy-start.2) | copy-done | bytes 262168
  3.5 9.4 %field_halo.1 = (bf16[2,3,32,256]{3,2,1,0:T(8,128)(2,1)S(1)}, bf16[2,3,16,256]{3,2,1,0:T(8,128)(2,1)S(1)}, bf16[2,2,3,16,256]{4,3,2,1,0:T(8,128)(2,1)S(1)}) custom-call(bf16[6,32,256]{2,1,0:T(8,128)(2,1)S(1)} %copy.16.edges, bf16[32,16,256]{2,1,0:T(8,128)(2,1)S(1)} %bitcast.11), custom_call_target="tpu_custom_call" | custom-call | tf_op jit(solution)/shard_map/field_halo/pallas_call | solution.py:149
  13.0 0.0 copy-start.3
  13.0 0.9 %copy-done.3 = bf16[1,32,16,256]{3,2,1,0:T(8,128)(2,1)S(1)} copy-done((bf16[1,32,16,256]{3,2,1,0:T(8,128)(2,1)S(1)}, bf16[1,32,16,256]{3,2,1,0:T(8,128)(2,1)}, u32[]{:S(2)}) %copy-start.3) | copy-done | bytes 262168
  13.9 0.0 copy-start.4
  13.9 1.2 %copy-done.4 = bf16[1024,512]{1,0:T(8,128)(2,1)S(1)} copy-done((bf16[1024,512]{1,0:T(8,128)(2,1)S(1)}, bf16[1024,512]{1,0:T(8,128)(2,1)}, u32[]{:S(2)}) %copy-start.4) | copy-done | bytes 1048600
  15.2 0.0 copy-start.5
  15.2 1.0 %copy-done.5 = bf16[256,1024]{1,0:T(8,128)(2,1)S(1)} copy-done((bf16[256,1024]{1,0:T(8,128)(2,1)S(1)}, bf16[256,1024]{1,0:T(8,128)(2,1)}, u32[]{:S(2)}) %copy-start.5) | copy-done | bytes 524312
  16.2 0.0 copy-start.6
  16.2 1.0 %copy-done.6 = bf16[1024,256]{1,0:T(8,128)(2,1)S(1)} copy-done((bf16[1024,256]{1,0:T(8,128)(2,1)S(1)}, bf16[1024,256]{1,0:T(8,128)(2,1)}, u32[]{:S(2)}) %copy-start.6) | copy-done | bytes 524312
  17.2 0.0 copy-start.7
  17.2 0.9 %copy-done.7 = bf16[1,16,8,512]{3,2,1,0:T(8,128)(2,1)S(1)} copy-done((bf16[1,16,8,512]{3,2,1,0:T(8,128)(2,1)S(1)}, bf16[1,16,8,512]{3,2,1,0:T(8,128)(2,1)}, u32[]{:S(2)}) %copy-start.7) | copy-done | bytes 131096
  18.2 0.0 copy-start.8
  18.2 0.7 copy-done.8
  18.8 0.0 copy-start.9
  18.8 0.7 copy-done.9
  19.5 9.9 %block.1 = (bf16[128,512]{1,0:T(8,128)(2,1)}, bf16[512,256]{1,0:T(8,128)(2,1)S(1)}, bf16[32,16,256]{2,1,0:T(8,128)(2,1)S(1)}, bf16[6,32,256]{2,1,0:T(8,128)(2,1)...) custom-call(bf16[32,16,256]{2,1,0:T(8,128)(2,1)S(1)} %bitcast.12, ...), custom_call_target="tpu_custom_call" | custom-call | tf_op jit(solution)/shard_map/block/pallas_call | solution.py:343
  29.4 0.0 copy-start.1
  29.4 1.6 %copy-done.1 = f32[1024,512]{1,0:T(8,128)S(1)} copy-done((f32[1024,512]{1,0:T(8,128)S(1)}, f32[1024,512]{1,0:T(8,128)}, u32[]{:S(2)}) %copy-start.1) | copy-done | bytes 2097176
  31.0 45.5 %sum_gradients.1 = (bf16[4608,256]{1,0:T(8,128)(2,1)}, bf16[2,3,32,256]{3,2,1,0:T(8,128)(2,1)S(1)}, bf16[2,3,16,256]{3,2,1,0:T(8,128)(2,1)S(1)}, bf16[2,2,3,16,256]{4,3,2,1,0:T(8,128)(2,1)S(1)}) custom-call(bf16[6,32,256]{2,1,0:T(8,128)(2,1)S(1)} %get-tuple-element.32.edges, bf16[32,16,256]{2,1,0:T(8,128)(2,1)S(1)} %get-tuple-element.33.cells, ...), custom_call_target="tpu_custom_call" | custom-call | tf_op jit(solution)/shard_map/sum_gradients/pallas_call | solution.py:530
  76.5 0.0 copy-start
  76.5 1.7 %copy-done = bf16[4608,256]{1,0:T(8,128)(2,1)S(1)} copy-done((bf16[4608,256]{1,0:T(8,128)(2,1)S(1)}, bf16[4608,256]{1,0:T(8,128)(2,1)}, u32[]{:S(2)}) %copy-start) | copy-done | bytes 2359320
  78.2 6.3 %finish.1 = (f32[256,1024]{1,0:T(8,128)}, f32[1024,256]{1,0:T(8,128)}, f32[1024,512]{1,0:T(8,128)}, f32[64,256]{1,0:T(8,128)S(1)}, bf16[512,256]{1,0:T(8,128)(2,1)}) custom-call(bf16[4608,256]{1,0:T(8,128)(2,1)S(1)} %copy-done, bf16[32,16,256]{2,1,0:T(8,128)(2,1)S(1)} %get-tuple-element.33.cells, bf16[2,3,32,256]{3,2,1,0:T(8,128)(2,1)S(1)} %get-tuple-element.39.side, ...), custom_call_target="tpu_custom_call" | custom-call | tf_op jit(solution)/shard_map/finish/pallas_call | solution.py:602
  84.4 0.6 fusion.1
  85.0 0.6 reshape.35
  (2 shorter events, 0.0 us)
Async XLA Ops:
  2.6 1.0 %copy-start.2 = (bf16[1,32,16,256]{3,2,1,0:T(8,128)(2,1)S(1)}, bf16[1,32,16,256]{3,2,1,0:T(8,128)(2,1)}, u32[]{:S(2)}) copy-start(bf16[1,32,16,256]{3,2,1,0:T(8,128)(2,1)} %param.8) | copy-start | bytes 786436
  13.0 1.0 %copy-start.3 = (bf16[1,32,16,256]{3,2,1,0:T(8,128)(2,1)S(1)}, bf16[1,32,16,256]{3,2,1,0:T(8,128)(2,1)}, u32[]{:S(2)}) copy-start(bf16[1,32,16,256]{3,2,1,0:T(8,128)(2,1)} %param.8) | copy-start | bytes 786436
  13.9 1.2 %copy-start.4 = (bf16[1024,512]{1,0:T(8,128)(2,1)S(1)}, bf16[1024,512]{1,0:T(8,128)(2,1)}, u32[]{:S(2)}) copy-start(bf16[1024,512]{1,0:T(8,128)(2,1)} %down.1) | copy-start | bytes 3145732
  15.2 1.0 %copy-start.5 = (bf16[256,1024]{1,0:T(8,128)(2,1)S(1)}, bf16[256,1024]{1,0:T(8,128)(2,1)}, u32[]{:S(2)}) copy-start(bf16[256,1024]{1,0:T(8,128)(2,1)} %inner.1) | copy-start | bytes 1572868
  16.2 1.0 %copy-start.6 = (bf16[1024,256]{1,0:T(8,128)(2,1)S(1)}, bf16[1024,256]{1,0:T(8,128)(2,1)}, u32[]{:S(2)}) copy-start(bf16[1024,256]{1,0:T(8,128)(2,1)} %outer.1) | copy-start | bytes 1572868
  17.2 0.9 %copy-start.7 = (bf16[1,16,8,512]{3,2,1,0:T(8,128)(2,1)S(1)}, bf16[1,16,8,512]{3,2,1,0:T(8,128)(2,1)}, u32[]{:S(2)}) copy-start(bf16[1,16,8,512]{3,2,1,0:T(8,128)(2,1)} %param.15) | copy-start | bytes 393220
  18.2 0.7 copy-start.8
  18.8 0.7 copy-start.9
  29.4 1.6 %copy-start.1 = (f32[1024,512]{1,0:T(8,128)S(1)}, f32[1024,512]{1,0:T(8,128)}, u32[]{:S(2)}) copy-start(f32[1024,512]{1,0:T(8,128)} %get-tuple-element.36.down) | copy-start | bytes 6291460
  76.5 1.7 %copy-start = (bf16[4608,256]{1,0:T(8,128)(2,1)S(1)}, bf16[4608,256]{1,0:T(8,128)(2,1)}, u32[]{:S(2)}) copy-start(bf16[4608,256]{1,0:T(8,128)(2,1)} %get-tuple-element.38.sums) | copy-start | bytes 7077892

commit v3 on v2

--- a/solution.py
+++ b/solution.py
@@ -149,6 +149,7 @@
     return pl.pallas_call(
         partial(halo_body, (mesh_shape["lon"], mesh_shape["lat"])),
         name="field_halo",
+        cost_estimate=pl.CostEstimate(flops=0, bytes_accessed=16 << 20, transcendentals=0),
         out_shape=halo_shapes(cells),
         in_specs=[VMEM_SPEC] * 2,
         out_specs=[VMEM_SPEC] * 3,
@@ -216,10 +217,11 @@
 
 
 def block_body(
-    cells, side, ends, corner, kernel, gain, inner, outer, scale, down, cotangent,
-    coarse, grad_cells, grad_depth, grad_edges, raw_inner, raw_outer, raw_down, small,
+    cells, side, ends, corner, kernel, gain, scale, inner, outer, down, cotangent,
+    coarse, grad_cells, grad_depth, grad_edges, packed,
     wide, shifted, mixed, grad_wide, blocked, normed, hidden, grad_pre, grad_branch, terms,
 ):
+    extend(cells, side, ends, corner, wide, shifted)
     rows, cols, channels = cells.shape
     f32, bf16 = jnp.float32, jnp.bfloat16
     cot = cotangent[...]
@@ -233,8 +235,6 @@
                 for lane in range(2):
                     grad_wide[lane, pl.ds(first, pair, stride=2), :] = gp[i * pair : (i + 1) * pair, HALVES[lane]]
 
-    extend(cells, side, ends, corner, wide, shifted)
-
     def convolve(t, carry):
         first = t * 8
         out = spread_rows(shifted, kernel, first, 8, False)
@@ -243,7 +243,8 @@
 
     lax.fori_loop(0, rows // 8, convolve, 0)
 
-    small[...] = jnp.zeros(small.shape, f32)
+    small = packed.at[4096:4160]
+    packed[4096:, :] = jnp.zeros((packed.shape[0] - 4096, channels), f32)
     chunk = 16 * cols
     g = gain[...]
     ls = scale[...]
@@ -291,8 +292,10 @@
     raw_gain, raw_scale = lax.fori_loop(0, rows // 16, step, (zero, zero))
     small[49:50, :] = raw_gain
     small[50:51, :] = raw_scale
-    raw_outer[...] = dot(hidden[...], grad_branch[...], (0, 0))
-    raw_inner[...] = dot(normed[...], grad_pre[...], (0, 0))
+    packed[1024:2048, :] = dot(hidden[...], grad_branch[...], (0, 0))
+    for c in range(4):
+        lanes = slice(c * 256, (c + 1) * 256)
+        packed[lanes, :] = dot(normed[...], grad_pre[:, lanes], (0, 0))
     total = None
     for p in range(2):
         for q in range(2):
@@ -310,7 +313,9 @@
             patch = jnp.concatenate(lanes, axis=1)
             part = dot(patch, down[at : at + channels, :], (1, 0))
             total = part if total is None else total + part
-            raw_down[at : at + channels, :] = dot(patch, cot, (0, 0))
+            raw = dot(patch, cot, (0, 0))
+            packed[2048 + at : 2048 + at + channels, :] = raw[:, 0:256]
+            packed[3072 + at : 3072 + at + channels, :] = raw[:, 256:512]
     coarse[...] = total.astype(bf16)
 
     terms[...] = jnp.zeros(terms.shape, f32)
@@ -335,7 +340,7 @@
                 ].astype(bf16)
 
 
-def block(cells, halos, kernel, gain, inner, outer, scale, down, cotangent):
+def block(cells, halos, kernel, gain, scale, inner, outer, down, cotangent, packed_rows):
     rows, cols, channels = cells.shape
     count = rows * cols
     hid = inner.shape[1]
@@ -343,18 +348,16 @@
     return pl.pallas_call(
         block_body,
         name="block",
+        cost_estimate=pl.CostEstimate(flops=0, bytes_accessed=32 << 20, transcendentals=0),
         out_shape=[
             jax.ShapeDtypeStruct(cotangent.shape, bf16),
             jax.ShapeDtypeStruct((count, channels), bf16),
             jax.ShapeDtypeStruct(cells.shape, bf16),
             jax.ShapeDtypeStruct((6, rows, channels), bf16),
-            jax.ShapeDtypeStruct(inner.shape, f32),
-            jax.ShapeDtypeStruct(outer.shape, f32),
-            jax.ShapeDtypeStruct(down.shape, f32),
-            jax.ShapeDtypeStruct((64, channels), f32),
+            jax.ShapeDtypeStruct((packed_rows, channels), f32),
         ],
         in_specs=[VMEM_SPEC] * 11,
-        out_specs=[VMEM_SPEC] * 8,
+        out_specs=[VMEM_SPEC] * 5,
         scratch_shapes=[
             pltpu.VMEM((2, (rows + 6) * 32, channels // 2), f32),
             pltpu.VMEM((7, rows + 6, cols, channels), f32),
@@ -367,185 +370,182 @@
             pltpu.VMEM((count, channels), bf16),
             pltpu.VMEM((49, 8, channels), f32),
         ],
-        compiler_params=pltpu.CompilerParams(vmem_limit_bytes=48 << 20),
-    )(cells, *halos, kernel, gain, inner, outer, scale, down, cotangent)
+        compiler_params=pltpu.CompilerParams(vmem_limit_bytes=36 << 20),
+    )(cells, *halos, kernel, gain, scale, inner, outer, down, cotangent)
 
 
 def place(mesh_shape):
     lon_bits = mesh_shape["lon"].bit_length() - 1
     lat_bits = mesh_shape["lat"].bit_length() - 1
-    core = ("lon", 0)
-    groups = [
-        [("lat", k) for k in range(lat_bits)],
-        [("lon", k) for k in range(1, min(2, lon_bits))],
-        [("lon", k) for k in range(2, lon_bits)],
+    core = [("lon", 0)]
+    plane = [("lat", k) for k in range(lat_bits)] + [("lon", k) for k in range(1, min(2, lon_bits))]
+    line = [("lon", k) for k in range(2, lon_bits)]
+    orders = [
+        [group for group in order if group]
+        for order in ([core, line, plane], [core, plane, line], [core, plane, line])
     ]
-    orders = []
-    for p in range(3):
-        rotated = groups[p:] + groups[:p]
-        orders.append([core] + [bit for group in rotated for bit in group])
     devices = mesh_shape["lon"] * mesh_shape["lat"]
     unit = 3 * 16 * devices
     rows = -(-(4096 + 64) // unit) * unit
     return orders, rows, devices
 
 
-def partner_of(bit):
-    axis, k = bit
-    me = lax.axis_index(axis)
-    b = lax.rem(lax.div(me, 2**k), 2)
-    return b, {axis: me + (1 - 2 * b) * 2**k}
+def peers_of(group):
+    bits = [lax.rem(lax.div(lax.axis_index(axis), 2**k), 2) for axis, k in group]
+    mine = sum(b * 2**n for n, b in enumerate(bits))
+    peers = []
+    for d in range(1, 2 ** len(group)):
+        where = {"lon": lax.axis_index("lon"), "lat": lax.axis_index("lat")}
+        index = mine
+        for n, (axis, k) in enumerate(group):
+            if d >> n & 1:
+                where[axis] = where[axis] + (1 - 2 * bits[n]) * 2**k
+                index = index + (1 - 2 * bits[n]) * 2**n
+        peers.append((index, where))
+    return mine, peers
 
 
 def sum_kernel_body(
-    orders, devices, sizes, edges, cells, inner, outer, down, small,
+    orders, devices, sizes, edges, cells, packed,
     out, side, ends, corner, acc, send, recv, ssem, rsem, halo_ssem, halo_rsem,
 ):
-    rows = acc.shape[0]
-    part_rows = rows // 3
+    part_rows = acc.shape[0] // 3
     stages = len(orders[0])
     barrier = pltpu.get_barrier_semaphore()
-    for bit in orders[0]:
-        _, device = partner_of(bit)
-        pl.semaphore_signal(barrier, inc=1, device_id=device, device_id_type=MESH)
+    count = 0
+    for group in orders[0]:
+        for _, device in peers_of(group)[1]:
+            pl.semaphore_signal(barrier, inc=1, device_id=device, device_id_type=MESH)
+            count += 1
     greet(barrier, sizes)
-
-    def pack_inner(i, carry):
-        r = pl.multiple_of(i * 64, 64)
-        for c in range(4):
-            acc[pl.ds(c * 256 + r, 64), :] = inner[pl.ds(r, 64), c * 256 : (c + 1) * 256]
-        return carry
-
-    lax.fori_loop(0, 4, pack_inner, 0)
-
-    def pack_rest(i, carry):
-        r = pl.multiple_of(i * 64, 64)
-        acc[pl.ds(1024 + r, 64), :] = outer[pl.ds(r, 64), :]
-        acc[pl.ds(2048 + r, 64), :] = down[pl.ds(r, 64), 0:256]
-        acc[pl.ds(3072 + r, 64), :] = down[pl.ds(r, 64), 256:512]
-        return carry
-
-    lax.fori_loop(0, 16, pack_rest, 0)
-    acc[4096:4160, :] = small[...]
-
-    def clear(i, carry):
-        acc[pl.ds(pl.multiple_of(4160 + i * 32, 32), 32), :] = jnp.zeros((32, 256), jnp.float32)
-        return carry
-
-    lax.fori_loop(0, (rows - 4160) // 32, clear, 0)
-    await_greetings(barrier, sizes, stages)
+    await_greetings(barrier, sizes, count)
     exchange_start(edges, cells, side, ends, corner, halo_ssem, halo_rsem, sizes)
 
-    unit = part_rows // devices
     offs = [p * part_rows for p in range(3)]
-    keeps = [[None] * stages for _ in range(3)]
+    lens = [part_rows] * 3
+    bases = [p * part_rows for p in range(3)]
+    slots = [0] * 3
+    owned = [[] for _ in range(3)]
     sent = []
 
-    def start(s, p):
-        b, device = partner_of(orders[p][s])
-        half = part_rows >> (s + 1)
-        base = p * part_rows + part_rows - 2 * half
-        away = offs[p] + (1 - b) * half
-        keeps[p][s] = offs[p] + b * half
-        chunk = min(half, 4 * unit)
-
-        def cast(i, carry):
-            r = i * chunk
-            send[pl.ds(pl.multiple_of(base + r, 16), chunk), :] = acc[
-                pl.ds(pl.multiple_of(away + r, 16), chunk), :
-            ].astype(jnp.bfloat16)
-            return carry
-
-        lax.fori_loop(0, half // chunk, cast, 0)
+    def piece(at, size):
+        return pl.ds(pl.multiple_of(at, 16), size)
+
+    def transfer(p, src, dst, device):
         copy = pltpu.make_async_remote_copy(
-            src_ref=send.at[pl.ds(base, half)],
-            dst_ref=recv.at[pl.ds(base, half)],
-            send_sem=ssem.at[p, s],
-            recv_sem=rsem.at[p, s],
+            src_ref=src,
+            dst_ref=dst,
+            send_sem=ssem.at[p, slots[p]],
+            recv_sem=rsem.at[p, slots[p]],
             device_id=device,
             device_id_type=MESH,
         )
         copy.start()
+        slots[p] += 1
         sent.append(copy)
         return copy
 
-    def finish(s, p, copy):
-        half = part_rows >> (s + 1)
-        base = p * part_rows + part_rows - 2 * half
-        keep = keeps[p][s]
-        chunk = min(half, 4 * unit)
-        copy.wait_recv()
+    def step_of(size):
+        return next(n for n in (192, 128, 96, 64, 48, 32, 16) if size % n == 0)
+
+    def start(s, p):
+        mine, peers = peers_of(orders[p][s])
+        size = lens[p] // (len(peers) + 1)
+        source = packed if s == 0 else acc
+        step = step_of(size)
+        copies = []
+        for n, (index, device) in enumerate(peers):
+            base = bases[p] + n * size
+            away = offs[p] + index * size
+
+            def cast(i, carry):
+                send[piece(base + i * step, step), :] = source[
+                    piece(away + i * step, step), :
+                ].astype(jnp.bfloat16)
+                return carry
+
+            lax.fori_loop(0, size // step, cast, 0)
+            copies.append(
+                transfer(p, send.at[pl.ds(base, size)], recv.at[pl.ds(base, size)], device)
+            )
+        return copies
+
+    def finish(s, p, copies):
+        mine, peers = peers_of(orders[p][s])
+        size = lens[p] // (len(peers) + 1)
+        base = bases[p]
+        keep = offs[p] + mine * size
+        source = packed if s == 0 else acc
+        step = min(64, step_of(size))
+        step = step if size % step == 0 else 16
+        for copy in copies:
+            copy.wait_recv()
 
         def add(i, carry):
-            r = i * chunk
-            mine = pl.ds(pl.multiple_of(keep + r, 16), chunk)
-            acc[mine, :] = acc[mine, :] + recv[
-                pl.ds(pl.multiple_of(base + r, 16), chunk), :
-            ].astype(jnp.float32)
+            here = piece(keep + i * step, step)
+            total = source[here, :]
+            for n in range(len(peers)):
+                total = total + recv[piece(base + n * size + i * step, step), :].astype(jnp.float32)
+            if s + 1 < stages:
+                acc[here, :] = total
+            else:
+                out[here, :] = total.astype(jnp.bfloat16)
             return carry
 
-        lax.fori_loop(0, half // chunk, add, 0)
-        offs[p] = keep
+        lax.fori_loop(0, size // step, add, 0)
+        owned[p].append((keep, size))
+        bases[p] += len(peers) * size
+        offs[p], lens[p] = keep, size
 
     def spread(s, p):
-        _, device = partner_of(orders[p][s])
-        half = part_rows >> (s + 1)
-        mine = pl.ds(pl.multiple_of(keeps[p][s], 16), half)
-        copy = pltpu.make_async_remote_copy(
-            src_ref=out.at[mine],
-            dst_ref=out.at[mine],
-            send_sem=ssem.at[p, stages + s],
-            recv_sem=rsem.at[p, stages + s],
-            device_id=device,
-            device_id_type=MESH,
-        )
-        copy.start()
-        sent.append(copy)
-        return copy
+        keep, size = owned[p][s]
+        mine = piece(keep, size)
+        return [
+            transfer(p, out.at[mine], out.at[mine], device)
+            for _, device in peers_of(orders[p][s])[1]
+        ]
 
     flight = [start(0, p) for p in range(3)]
     for s in range(stages):
         for p in range(3):
             finish(s, p, flight[p])
-            if s + 1 < stages:
-                flight[p] = start(s + 1, p)
-            else:
-                mine = pl.ds(pl.multiple_of(offs[p], 16), unit)
-                out[mine, :] = acc[mine, :].astype(jnp.bfloat16)
-                flight[p] = spread(stages - 1, p)
+            flight[p] = start(s + 1, p) if s + 1 < stages else spread(s, p)
     for s in range(stages - 2, -1, -1):
         for p in range(3):
-            flight[p].wait_recv()
+            for copy in flight[p]:
+                copy.wait_recv()
             flight[p] = spread(s, p)
     for p in range(3):
-        flight[p].wait_recv()
+        for copy in flight[p]:
+            copy.wait_recv()
     for copy in sent:
         copy.wait_send()
     exchange_finish(edges, cells, side, ends, corner, halo_ssem, halo_rsem, sizes)
 
 
-def summed(edges, cells, inner, outer, down, small, mesh_shape):
+def summed(edges, cells, packed, mesh_shape):
     orders, rows, devices = place(mesh_shape)
-    stages = len(orders[0])
+    copies = 2 * sum(2 ** len(group) - 1 for group in orders[0])
     return pl.pallas_call(
         partial(sum_kernel_body, orders, devices, (mesh_shape["lon"], mesh_shape["lat"])),
         name="sum_gradients",
+        cost_estimate=pl.CostEstimate(flops=0, bytes_accessed=96 << 20, transcendentals=0),
         out_shape=[jax.ShapeDtypeStruct((rows, 256), jnp.bfloat16)] + halo_shapes(cells),
-        in_specs=[VMEM_SPEC] * 6,
+        in_specs=[VMEM_SPEC] * 3,
         out_specs=[VMEM_SPEC] * 4,
         scratch_shapes=[
             pltpu.VMEM((rows, 256), jnp.float32),
             pltpu.VMEM((rows, 256), jnp.bfloat16),
             pltpu.VMEM((rows, 256), jnp.bfloat16),
-            pltpu.SemaphoreType.DMA((3, 2 * stages)),
-            pltpu.SemaphoreType.DMA((3, 2 * stages)),
+            pltpu.SemaphoreType.DMA((3, copies)),
+            pltpu.SemaphoreType.DMA((3, copies)),
             pltpu.SemaphoreType.DMA((8,)),
             pltpu.SemaphoreType.DMA((8,)),
         ],
         compiler_params=pltpu.CompilerParams(
-            collective_id=1, has_side_effects=True, vmem_limit_bytes=48 << 20
+            collective_id=1, has_side_effects=True, vmem_limit_bytes=32 << 20
         ),
-    )(edges, cells, inner, outer, down, small)
+    )(edges, cells, packed)
 
 
 def finish_body(
@@ -602,6 +602,7 @@
     return pl.pallas_call(
         finish_body,
         name="finish",
+        cost_estimate=pl.CostEstimate(flops=0, bytes_accessed=16 << 20, transcendentals=0),
         out_shape=[jax.ShapeDtypeStruct(shape, f32) for shape in shapes]
         + [jax.ShapeDtypeStruct(grad_cells.shape, jnp.bfloat16)],
         in_specs=[VMEM_SPEC] * 7,
@@ -610,7 +611,7 @@
             pltpu.VMEM((2, (rows + 6) * 32, channels // 2), f32),
             pltpu.VMEM((7, rows + 6, cols, channels), f32),
         ],
-        compiler_params=pltpu.CompilerParams(vmem_limit_bytes=48 << 20),
+        compiler_params=pltpu.CompilerParams(vmem_limit_bytes=32 << 20),
     )(sums, cells, *halos, kernel, grad_cells)
 
 
@@ -630,20 +631,19 @@
     edges = jnp.concatenate([cells[:, :3], cells[:, cols - 3 :]], axis=1).transpose(1, 0, 2)
     kernel = depth_kernel.reshape(49, channels)
     halos = halo(edges, cells, mesh_shape)
-    coarse, grad_cells, grad_depth, grad_edges, raw_inner, raw_outer, raw_down, small = block(
+    coarse, grad_cells, grad_depth, grad_edges, packed = block(
         cells,
         halos,
         kernel,
         layer_norm_gain[None],
+        layer_scale[None],
         inner_weight,
         outer_weight,
-        layer_scale[None],
         down_weight,
         cotangent.reshape(-1, cotangent.shape[3]),
+        place(mesh_shape)[1],
     )
-    sums, *grad_halos = summed(
-        grad_edges, grad_depth, raw_inner, raw_outer, raw_down, small, mesh_shape
-    )
+    sums, *grad_halos = summed(grad_edges, grad_depth, packed, mesh_shape)
     grad_inner, grad_outer, grad_down, grad_small, grad_field = finished(
         sums, grad_depth, grad_halos, kernel, grad_cells
     )

time: 86.1 us -> 71.5 us (0.83)
  Pallas kernels: 71.1 us -> 59.8 us
  local copies, waits for them, and re-layouts: 13.8 us -> 10.5 us
    pallas_call x1, Pallas kernels: 45.5 us -> 35.1 us  [summed(): pl.pallas_call(partial(sum_kernel_body, orders, devices, (mesh_shape['lon...]
    unnamed x20 -> x16, local copies, waits for them, and re-layouts: 10.7 us -> 7.46 us
where the time goes in v3:
time: 71.5 us; the launch traced here: 71.1 us
  Pallas kernels  59.8 us (84%)
  local copies, waits for them, and re-layouts  10.5 us (15%)
    pallas_call x1, Pallas kernels, summed(): pl.pallas_call(partial(sum_kernel_body, orders, devices, (mesh_shape['lon...  35.1 us
    pallas_call x1, Pallas kernels, halo(): pl.pallas_call(partial(halo_body, (mesh_shape['lon'], mesh_shape['lat']))...  9.43 us
    pallas_call x1, Pallas kernels, block(): pl.pallas_call(block_body, name='block', cost_estimate=pl.CostEstimate(fl...  8.99 us
    unnamed x16, local copies, waits for them, and re-layouts  7.46 us
    pallas_call x1, Pallas kernels, finished(): pl.pallas_call(finish_body, name='finish', cost_estimate=pl.CostEstimate(...  6.26 us

profile of v3, /device:TPU:0, one launch (start us, length us, event | category | flops | bytes accessed | tf_op | source)
XLA Modules:
  0.0 71.1 jit_solution(8977660806739702647)
XLA Ops:
  0.6 0.8 %reshape.31.kernel = f32[49,256]{1,0:T(8,128)S(1)} reshape(f32[7,7,256]{2,1,0:T(8,128)} %param.9) | data formatting | bytes 100352 | tf_op jit(solution)/shard_map/reshape | solution.py:632
  1.5 1.0 %fusion = (bf16[32,3,256]{2,1,0:T(4,128)(2,1)S(1)}, bf16[32,3,256]{2,1,0:T(4,128)(2,1)S(1)}) fusion(bf16[32,16,256]{2,1,0:T(8,128)(2,1)} %bitcast.10), kind=kLoop, calls=%fused_computation.1 | loop fusion | bytes 196608 | tf_op jit(solution)/shard_map/slice | solution.py:631
  2.5 0.1 maximum_bitcast_fusion
  2.6 0.0 copy-start
  2.6 0.9 %copy-done = bf16[1,32,16,256]{3,2,1,0:T(8,128)(2,1)S(1)} copy-done((bf16[1,32,16,256]{3,2,1,0:T(8,128)(2,1)S(1)}, bf16[1,32,16,256]{3,2,1,0:T(8,128)(2,1)}, u32[]{:S(2)}) %copy-start) | copy-done | bytes 262168
  3.5 9.4 %field_halo.1 = (bf16[2,3,32,256]{3,2,1,0:T(8,128)(2,1)S(1)}, bf16[2,3,16,256]{3,2,1,0:T(8,128)(2,1)S(1)}, bf16[2,2,3,16,256]{4,3,2,1,0:T(8,128)(2,1)S(1)}) custom-call(bf16[6,32,256]{2,1,0:T(8,128)(2,1)S(1)} %copy.16.edges, bf16[32,16,256]{2,1,0:T(8,128)(2,1)S(1)} %bitcast.11), custom_call_target="tpu_custom_call" | custom-call | bytes 16777216 | tf_op jit(solution)/shard_map/field_halo/pallas_call | solution.py:149
  13.0 0.0 copy-start.1
  13.0 0.9 %copy-done.1 = bf16[1,32,16,256]{3,2,1,0:T(8,128)(2,1)S(1)} copy-done((bf16[1,32,16,256]{3,2,1,0:T(8,128)(2,1)S(1)}, bf16[1,32,16,256]{3,2,1,0:T(8,128)(2,1)}, u32[]{:S(2)}) %copy-start.1) | copy-done | bytes 262168
  13.9 0.0 copy-start.2
  13.9 1.2 %copy-done.2 = bf16[1024,512]{1,0:T(8,128)(2,1)S(1)} copy-done((bf16[1024,512]{1,0:T(8,128)(2,1)S(1)}, bf16[1024,512]{1,0:T(8,128)(2,1)}, u32[]{:S(2)}) %copy-start.2) | copy-done | bytes 1048600
  15.2 0.0 copy-start.3
  15.2 1.0 %copy-done.3 = bf16[256,1024]{1,0:T(8,128)(2,1)S(1)} copy-done((bf16[256,1024]{1,0:T(8,128)(2,1)S(1)}, bf16[256,1024]{1,0:T(8,128)(2,1)}, u32[]{:S(2)}) %copy-start.3) | copy-done | bytes 524312
  16.2 0.0 copy-start.4
  16.2 1.0 %copy-done.4 = bf16[1024,256]{1,0:T(8,128)(2,1)S(1)} copy-done((bf16[1024,256]{1,0:T(8,128)(2,1)S(1)}, bf16[1024,256]{1,0:T(8,128)(2,1)}, u32[]{:S(2)}) %copy-start.4) | copy-done | bytes 524312
  17.2 0.0 copy-start.5
  17.2 0.9 %copy-done.5 = bf16[1,16,8,512]{3,2,1,0:T(8,128)(2,1)S(1)} copy-done((bf16[1,16,8,512]{3,2,1,0:T(8,128)(2,1)S(1)}, bf16[1,16,8,512]{3,2,1,0:T(8,128)(2,1)}, u32[]{:S(2)}) %copy-start.5) | copy-done | bytes 131096
  18.2 0.0 copy-start.6
  18.2 0.7 copy-done.6
  18.8 0.0 copy-start.7
  18.8 0.7 copy-done.7
  19.5 9.0 %block.1 = (bf16[128,512]{1,0:T(8,128)(2,1)}, bf16[512,256]{1,0:T(8,128)(2,1)S(1)}, bf16[32,16,256]{2,1,0:T(8,128)(2,1)S(1)}, bf16[6,32,256]{2,1,0:T(8,128)(2,1)S(1)}, f32[4608,256]{1,0:T(8,128)S(1)}) custom-call(bf16[32,16,256]{2,1,0:T(8,128)(2,1)S(1)} %bitcast.12, bf16[2,3,32,256]{3,2,1,0:T(8,128)(2,1)S(1)} %get-tuple-element.25.side, ...), custom_call_target="tpu_custom_call" | custom-call | bytes 33554432 | tf_op jit(solution)/shard_map/block/pallas_call | solution.py:348
  28.5 35.1 %sum_gradients.1 = (bf16[4608,256]{1,0:T(8,128)(2,1)S(1)}, bf16[2,3,32,256]{3,2,1,0:T(8,128)(2,1)S(1)}, bf16[2,3,16,256]{3,2,1,0:T(8,128)(2,1)S(1)}, bf16[2,2,3,16,256]{4,3,2,1,0:T(8,128)(2,1)S(1)}) custom-call(bf16[6,32,256]{2,1,0:T(8,128)(2,1)S(1)} %get-tuple-element.29.edges, bf16[32,16,256]{2,1,0:T(8,128)(2,1)S(1)} %get-tuple-element.30.cells, ...), custom_call_target="tpu_custom_call" | custom-call | bytes 100663296 | tf_op jit(solution)/shard_map/sum_gradients/pallas_call | solution.py:529
  63.6 6.3 %finish.1 = (f32[256,1024]{1,0:T(8,128)}, f32[1024,256]{1,0:T(8,128)}, f32[1024,512]{1,0:T(8,128)}, f32[64,256]{1,0:T(8,128)S(1)}, bf16[512,256]{1,0:T(8,128)(2,1)}) custom-call(bf16[4608,256]{1,0:T(8,128)(2,1)S(1)} %get-tuple-element.32.sums, bf16[32,16,256]{2,1,0:T(8,128)(2,1)S(1)} %get-tuple-element.30.cells, ...), custom_call_target="tpu_custom_call" | custom-call | bytes 16777216 | tf_op jit(solution)/shard_map/finish/pallas_call | solution.py:602
  69.9 0.6 fusion.1
  70.5 0.6 reshape.35
  (2 shorter events, 0.0 us)
Async XLA Ops:
  2.6 1.0 %copy-start = (bf16[1,32,16,256]{3,2,1,0:T(8,128)(2,1)S(1)}, bf16[1,32,16,256]{3,2,1,0:T(8,128)(2,1)}, u32[]{:S(2)}) copy-start(bf16[1,32,16,256]{3,2,1,0:T(8,128)(2,1)} %param.8) | copy-start | bytes 786436
  13.0 1.0 %copy-start.1 = (bf16[1,32,16,256]{3,2,1,0:T(8,128)(2,1)S(1)}, bf16[1,32,16,256]{3,2,1,0:T(8,128)(2,1)}, u32[]{:S(2)}) copy-start(bf16[1,32,16,256]{3,2,1,0:T(8,128)(2,1)} %param.8) | copy-start | bytes 786436
  13.9 1.2 %copy-start.2 = (bf16[1024,512]{1,0:T(8,128)(2,1)S(1)}, bf16[1024,512]{1,0:T(8,128)(2,1)}, u32[]{:S(2)}) copy-start(bf16[1024,512]{1,0:T(8,128)(2,1)} %down.1) | copy-start | bytes 3145732
  15.2 1.0 %copy-start.3 = (bf16[256,1024]{1,0:T(8,128)(2,1)S(1)}, bf16[256,1024]{1,0:T(8,128)(2,1)}, u32[]{:S(2)}) copy-start(bf16[256,1024]{1,0:T(8,128)(2,1)} %inner.1) | copy-start | bytes 1572868
  16.2 1.0 %copy-start.4 = (bf16[1024,256]{1,0:T(8,128)(2,1)S(1)}, bf16[1024,256]{1,0:T(8,128)(2,1)}, u32[]{:S(2)}) copy-start(bf16[1024,256]{1,0:T(8,128)(2,1)} %outer.1) | copy-start | bytes 1572868
  17.2 0.9 %copy-start.5 = (bf16[1,16,8,512]{3,2,1,0:T(8,128)(2,1)S(1)}, bf16[1,16,8,512]{3,2,1,0:T(8,128)(2,1)}, u32[]{:S(2)}) copy-start(bf16[1,16,8,512]{3,2,1,0:T(8,128)(2,1)} %param.15) | copy-start | bytes 393220
  18.2 0.7 copy-start.6
  18.8 0.7 copy-start.7

commit v4 on v3

--- a/solution.py
+++ b/solution.py
@@ -124,14 +124,6 @@
         corner[1] = jnp.zeros(corner.shape[1:], corner.dtype)
 
 
-def halo_body(sizes, edges, cells, side, ends, corner, ssem, rsem):
-    barrier = pltpu.get_barrier_semaphore()
-    greet(barrier, sizes)
-    await_greetings(barrier, sizes, 0)
-    exchange_start(edges, cells, side, ends, corner, ssem, rsem, sizes)
-    exchange_finish(edges, cells, side, ends, corner, ssem, rsem, sizes)
-
-
 def halo_shapes(cells):
     rows, cols, channels = cells.shape
     return [
@@ -143,40 +135,38 @@
 
 HALVES = (slice(0, 128), slice(128, 256))
 VMEM_SPEC = pl.BlockSpec(memory_space=pltpu.VMEM)
-
-
-def halo(edges, cells, mesh_shape):
-    return pl.pallas_call(
-        partial(halo_body, (mesh_shape["lon"], mesh_shape["lat"])),
-        name="field_halo",
-        cost_estimate=pl.CostEstimate(flops=0, bytes_accessed=16 << 20, transcendentals=0),
-        out_shape=halo_shapes(cells),
-        in_specs=[VMEM_SPEC] * 2,
-        out_specs=[VMEM_SPEC] * 3,
-        scratch_shapes=[pltpu.SemaphoreType.DMA((8,)), pltpu.SemaphoreType.DMA((8,))],
-        compiler_params=pltpu.CompilerParams(
-            collective_id=0, has_side_effects=True, vmem_limit_bytes=8 << 20
-        ),
-    )(edges, cells)
+FAR_SPEC = pl.BlockSpec(memory_space=pltpu.HBM)
+
+
+def fetched(far, near, sems):
+    copies = [pltpu.make_async_copy(f, n, sems.at[k]) for k, (f, n) in enumerate(zip(far, near))]
+    for copy in copies:
+        copy.start()
+    return copies
+
+
+def put(wide, where, values):
+    values = values.astype(jnp.float32)
+    for h in range(2):
+        wide[h, where, :] = values[:, HALVES[h]]
+
+
+def fill_inside(cells, wide):
+    rows, cols, _ = cells.shape
+
+    def fill(r, carry):
+        put(wide, pl.ds(pl.multiple_of((3 + r) * 32 + 8, 8), cols), cells[r])
+        return carry
+
+    lax.fori_loop(0, rows, fill, 0)
 
 
 def extend(cells, side, ends, corner, wide, shifted):
     rows, cols, _ = cells.shape
     f32 = jnp.float32
-
-    def put(where, values):
-        values = values.astype(f32)
-        for h in range(2):
-            wide[h, where, :] = values[:, HALVES[h]]
-
-    def fill(r, carry):
-        put(pl.ds(pl.multiple_of((3 + r) * 32 + 8, 8), cols), cells[r])
-        return carry
-
-    lax.fori_loop(0, rows, fill, 0)
     for r in range(3):
-        put(pl.ds(r * 32 + 8, cols), ends[0, r])
-        put(pl.ds((rows + 3 + r) * 32 + 8, cols), ends[1, r])
+        put(wide, pl.ds(r * 32 + 8, cols), ends[0, r])
+        put(wide, pl.ds((rows + 3 + r) * 32 + 8, cols), ends[1, r])
     for h in range(2):
         for s, first in ((0, 5), (1, 8 + cols)):
             for c in range(3):
@@ -189,8 +179,8 @@
             high = corner[0, s, c].astype(f32)
             low = corner[1, s, c].astype(f32)
             for r in range(3):
-                put(pl.ds(r * 32 + first + c, 1), high[13 + r : 14 + r])
-                put(pl.ds((rows + 3 + r) * 32 + first + c, 1), low[r : r + 1])
+                put(wide, pl.ds(r * 32 + first + c, 1), high[13 + r : 14 + r])
+                put(wide, pl.ds((rows + 3 + r) * 32 + first + c, 1), low[r : r + 1])
 
     def shift(r, carry):
         for h in range(2):
@@ -206,8 +196,8 @@
     total = None
     for q in range(7):
         for p in range(7):
-            at = (6 - p) * 7 + (6 - q) if flip else p * 7 + q
-            term = shifted[q, pl.ds(first + p, count)] * kernel[at : at + 1, :]
+            i, j = (6 - p, 6 - q) if flip else (p, q)
+            term = shifted[q, pl.ds(first + p, count)] * kernel[i, j : j + 1, :]
             total = term if total is None else total + term
     return total
 
@@ -216,14 +206,42 @@
     return lax.dot_general(a, b, ((contract[0:1], contract[1:2]), ((), ())), preferred_element_type=jnp.float32)
 
 
-def block_body(
-    cells, side, ends, corner, kernel, gain, scale, inner, outer, down, cotangent,
-    coarse, grad_cells, grad_depth, grad_edges, packed,
+def main_body(
+    orders, devices, sizes,
+    cells_far, kernel_far, gain_far, scale_far, inner_far, outer_far, down_far, cotangent_far,
+    coarse, grad_cells, grad_depth, sums, grad_side, grad_ends, grad_corner,
+    cells, kernel, gain, scale, inner, outer, down, cotangent, loads,
+    edges, side, ends, corner, grad_edges, packed,
     wide, shifted, mixed, grad_wide, blocked, normed, hidden, grad_pre, grad_branch, terms,
+    acc, send, recv, ssem, rsem, first_ssem, first_rsem, second_ssem, second_rsem,
 ):
-    extend(cells, side, ends, corner, wide, shifted)
+    barrier = pltpu.get_barrier_semaphore()
+    count = 0
+    for group in orders[0]:
+        for _, device in peers_of(group)[1]:
+            pl.semaphore_signal(barrier, inc=1, device_id=device, device_id_type=MESH)
+            count += 1
+    greet(barrier, sizes)
+    loading = fetched(
+        (cells_far, kernel_far, gain_far, scale_far, cotangent_far, down_far, inner_far, outer_far),
+        (cells, kernel, gain, scale, cotangent, down, inner, outer),
+        loads,
+    )
     rows, cols, channels = cells.shape
     f32, bf16 = jnp.float32, jnp.bfloat16
+    loading[0].wait()
+    fill_inside(cells, wide)
+    for h in range(2):
+        for c in range(3):
+            for at, column in ((c, c), (3 + c, cols - 3 + c)):
+                edges[at, :, HALVES[h]] = wide[
+                    h, pl.ds(3 * 32 + 8 + column, rows, stride=32), :
+                ].astype(bf16)
+    await_greetings(barrier, sizes, count)
+    exchange_start(edges, cells, side, ends, corner, first_ssem, first_rsem, sizes)
+    for copy in loading[1:]:
+        copy.wait()
+    adding = sum_steps(orders, packed, sums, acc, send, recv, ssem, rsem)
     cot = cotangent[...]
     pair = cols // 2
     for p in range(2):
@@ -234,6 +252,9 @@
                 first = (2 * i + p) * cols + q
                 for lane in range(2):
                     grad_wide[lane, pl.ds(first, pair, stride=2), :] = gp[i * pair : (i + 1) * pair, HALVES[lane]]
+
+    exchange_finish(edges, cells, side, ends, corner, first_ssem, first_rsem, sizes)
+    extend(cells, side, ends, corner, wide, shifted)
 
     def convolve(t, carry):
         first = t * 8
@@ -292,10 +313,20 @@
     raw_gain, raw_scale = lax.fori_loop(0, rows // 16, step, (zero, zero))
     small[49:50, :] = raw_gain
     small[50:51, :] = raw_scale
+    for h in range(2):
+        for c in range(3):
+            for at, column in ((c, c), (3 + c, cols - 3 + c)):
+                grad_edges[at, :, HALVES[h]] = grad_wide[
+                    h, pl.ds(column, rows, stride=cols), :
+                ].astype(bf16)
+    exchange_start(
+        grad_edges, grad_depth, grad_side, grad_ends, grad_corner, second_ssem, second_rsem, sizes
+    )
     packed[1024:2048, :] = dot(hidden[...], grad_branch[...], (0, 0))
     for c in range(4):
         lanes = slice(c * 256, (c + 1) * 256)
         packed[lanes, :] = dot(normed[...], grad_pre[:, lanes], (0, 0))
+    next(adding)
     total = None
     for p in range(2):
         for q in range(2):
@@ -317,6 +348,7 @@
             packed[2048 + at : 2048 + at + channels, :] = raw[:, 0:256]
             packed[3072 + at : 3072 + at + channels, :] = raw[:, 256:512]
     coarse[...] = total.astype(bf16)
+    next(adding)
 
     terms[...] = jnp.zeros(terms.shape, f32)
 
@@ -332,33 +364,44 @@
 
     lax.fori_loop(0, rows // 4, kernel_step, 0)
     small[0:49, :] = jnp.sum(terms[...], axis=1)
-    for h in range(2):
-        for c in range(3):
-            for at, column in ((c, c), (3 + c, cols - 3 + c)):
-                grad_edges[at, :, HALVES[h]] = grad_wide[
-                    h, pl.ds(column, rows, stride=cols), :
-                ].astype(bf16)
-
-
-def block(cells, halos, kernel, gain, scale, inner, outer, down, cotangent, packed_rows):
+    next(adding)
+    for _ in adding:
+        pass
+    exchange_finish(
+        grad_edges, grad_depth, grad_side, grad_ends, grad_corner, second_ssem, second_rsem, sizes
+    )
+
+
+def main(cells, kernel, gain, scale, inner, outer, down, cotangent, mesh_shape):
     rows, cols, channels = cells.shape
     count = rows * cols
     hid = inner.shape[1]
     f32, bf16 = jnp.float32, jnp.bfloat16
+    orders, packed_rows, devices = place(mesh_shape)
+    copies = 2 * sum(2 ** len(group) - 1 for group in orders[0])
+    operands = (cells, kernel, gain, scale, inner, outer, down, cotangent)
+    sizes = (mesh_shape["lon"], mesh_shape["lat"])
     return pl.pallas_call(
-        block_body,
-        name="block",
-        cost_estimate=pl.CostEstimate(flops=0, bytes_accessed=32 << 20, transcendentals=0),
+        partial(main_body, orders, devices, sizes),
+        name="main",
         out_shape=[
             jax.ShapeDtypeStruct(cotangent.shape, bf16),
             jax.ShapeDtypeStruct((count, channels), bf16),
             jax.ShapeDtypeStruct(cells.shape, bf16),
-            jax.ShapeDtypeStruct((6, rows, channels), bf16),
-            jax.ShapeDtypeStruct((packed_rows, channels), f32),
-        ],
-        in_specs=[VMEM_SPEC] * 11,
-        out_specs=[VMEM_SPEC] * 5,
-        scratch_shapes=[
+            jax.ShapeDtypeStruct((packed_rows, channels), bf16),
+        ]
+        + halo_shapes(cells),
+        in_specs=[FAR_SPEC] * 8,
+        out_specs=[VMEM_SPEC] * 7,
+        scratch_shapes=[pltpu.VMEM(x.shape, x.dtype) for x in operands]
+        + [
+            pltpu.SemaphoreType.DMA((8,)),
+            pltpu.VMEM((6, rows, channels), bf16),
+        ]
+        + [pltpu.VMEM(x.shape, x.dtype) for x in halo_shapes(cells)]
+        + [
+            pltpu.VMEM((6, rows, channels), bf16),
+            pltpu.VMEM((packed_rows, channels), f32),
             pltpu.VMEM((2, (rows + 6) * 32, channels // 2), f32),
             pltpu.VMEM((7, rows + 6, cols, channels), f32),
             pltpu.VMEM((count, channels), f32),
@@ -369,9 +412,17 @@
             pltpu.VMEM((count, hid), bf16),
             pltpu.VMEM((count, channels), bf16),
             pltpu.VMEM((49, 8, channels), f32),
-        ],
-        compiler_params=pltpu.CompilerParams(vmem_limit_bytes=36 << 20),
-    )(cells, *halos, kernel, gain, scale, inner, outer, down, cotangent)
+            pltpu.VMEM((packed_rows, channels), f32),
+            pltpu.VMEM((packed_rows, channels), bf16),
+            pltpu.VMEM((packed_rows, channels), bf16),
+            pltpu.SemaphoreType.DMA((3, copies)),
+            pltpu.SemaphoreType.DMA((3, copies)),
+        ]
+        + [pltpu.SemaphoreType.DMA((8,))] * 4,
+        compiler_params=pltpu.CompilerParams(
+            collective_id=0, has_side_effects=True, vmem_limit_bytes=58 << 20
+        ),
+    )(*operands)
 
 
 def place(mesh_shape):
@@ -405,22 +456,9 @@
     return mine, peers
 
 
-def sum_kernel_body(
-    orders, devices, sizes, edges, cells, packed,
-    out, side, ends, corner, acc, send, recv, ssem, rsem, halo_ssem, halo_rsem,
-):
+def sum_steps(orders, packed, out, acc, send, recv, ssem, rsem):
     part_rows = acc.shape[0] // 3
     stages = len(orders[0])
-    barrier = pltpu.get_barrier_semaphore()
-    count = 0
-    for group in orders[0]:
-        for _, device in peers_of(group)[1]:
-            pl.semaphore_signal(barrier, inc=1, device_id=device, device_id_type=MESH)
-            count += 1
-    greet(barrier, sizes)
-    await_greetings(barrier, sizes, count)
-    exchange_start(edges, cells, side, ends, corner, halo_ssem, halo_rsem, sizes)
-
     offs = [p * part_rows for p in range(3)]
     lens = [part_rows] * 3
     bases = [p * part_rows for p in range(3)]
@@ -505,7 +543,10 @@
             for _, device in peers_of(orders[p][s])[1]
         ]
 
-    flight = [start(0, p) for p in range(3)]
+    flight = []
+    for p in range(3):
+        flight.append(start(0, p))
+        yield
     for s in range(stages):
         for p in range(3):
             finish(s, p, flight[p])
@@ -520,38 +561,34 @@
             copy.wait_recv()
     for copy in sent:
         copy.wait_send()
-    exchange_finish(edges, cells, side, ends, corner, halo_ssem, halo_rsem, sizes)
-
-
-def summed(edges, cells, packed, mesh_shape):
-    orders, rows, devices = place(mesh_shape)
-    copies = 2 * sum(2 ** len(group) - 1 for group in orders[0])
-    return pl.pallas_call(
-        partial(sum_kernel_body, orders, devices, (mesh_shape["lon"], mesh_shape["lat"])),
-        name="sum_gradients",
-        cost_estimate=pl.CostEstimate(flops=0, bytes_accessed=96 << 20, transcendentals=0),
-        out_shape=[jax.ShapeDtypeStruct((rows, 256), jnp.bfloat16)] + halo_shapes(cells),
-        in_specs=[VMEM_SPEC] * 3,
-        out_specs=[VMEM_SPEC] * 4,
-        scratch_shapes=[
-            pltpu.VMEM((rows, 256), jnp.float32),
-            pltpu.VMEM((rows, 256), jnp.bfloat16),
-            pltpu.VMEM((rows, 256), jnp.bfloat16),
-            pltpu.SemaphoreType.DMA((3, copies)),
-            pltpu.SemaphoreType.DMA((3, copies)),
-            pltpu.SemaphoreType.DMA((8,)),
-            pltpu.SemaphoreType.DMA((8,)),
-        ],
-        compiler_params=pltpu.CompilerParams(
-            collective_id=1, has_side_effects=True, vmem_limit_bytes=32 << 20
-        ),
-    )(edges, cells, packed)
 
 
 def finish_body(
-    sums, cells, side, ends, corner, kernel, grad_cells,
-    inner, outer, down, small, grad_field, wide, shifted,
+    sums_far, cells_far, side_far, ends_far, corner_far, kernel_far, grad_cells_far,
+    inner, outer, down, grad_kernel, gain, scale, grad_field,
+    sums, cells, side, ends, corner, kernel, grad_cells, loads, wide, shifted,
 ):
+    loading = fetched(
+        (cells_far, side_far, ends_far, corner_far, kernel_far, grad_cells_far, sums_far),
+        (cells, side, ends, corner, kernel, grad_cells, sums),
+        loads,
+    )
+    for copy in loading[:6]:
+        copy.wait()
+    fill_inside(cells, wide)
+    extend(cells, side, ends, corner, wide, shifted)
+    rows, cols, channels = cells.shape
+
+    def convolve(t, carry):
+        first = t * 8
+        here = pl.ds(pl.multiple_of(first * cols, 128), 8 * cols)
+        out = spread_rows(shifted, kernel, first, 8, True).reshape(8 * cols, channels)
+        grad_field[here, :] = (grad_cells[here, :].astype(jnp.float32) + out).astype(jnp.bfloat16)
+        return carry
+
+    lax.fori_loop(0, rows // 8, convolve, 0)
+    loading[6].wait()
+
     def squares(i, total):
         v = sums[pl.ds(pl.multiple_of(i * 64, 64), 64), :].astype(jnp.float32)
         v = v * v
@@ -581,38 +618,33 @@
         return carry
 
     lax.fori_loop(0, 16, write_rest, 0)
-    small[...] = sums[4096:4160, :].astype(jnp.float32) * factor
-    rows, cols, channels = cells.shape
-    extend(cells, side, ends, corner, wide, shifted)
-
-    def convolve(t, carry):
-        first = t * 8
-        here = pl.ds(pl.multiple_of(first * cols, 128), 8 * cols)
-        out = spread_rows(shifted, kernel, first, 8, True).reshape(8 * cols, channels)
-        grad_field[here, :] = (grad_cells[here, :].astype(jnp.float32) + out).astype(jnp.bfloat16)
-        return carry
-
-    lax.fori_loop(0, rows // 8, convolve, 0)
+    last = sums[4096:4160, :].astype(jnp.float32) * factor
+    for p in range(7):
+        grad_kernel[p] = last[7 * p : 7 * p + 7]
+    gain[...] = last[49:50]
+    scale[...] = last[50:51]
 
 
 def finished(sums, cells, halos, kernel, grad_cells):
     rows, cols, channels = cells.shape
     f32 = jnp.float32
-    shapes = ((256, 1024), (1024, 256), (1024, 512), (64, 256))
+    shapes = ((256, 1024), (1024, 256), (1024, 512), kernel.shape, (1, channels), (1, channels))
+    operands = (sums, cells, *halos, kernel, grad_cells)
     return pl.pallas_call(
         finish_body,
         name="finish",
-        cost_estimate=pl.CostEstimate(flops=0, bytes_accessed=16 << 20, transcendentals=0),
         out_shape=[jax.ShapeDtypeStruct(shape, f32) for shape in shapes]
         + [jax.ShapeDtypeStruct(grad_cells.shape, jnp.bfloat16)],
-        in_specs=[VMEM_SPEC] * 7,
-        out_specs=[VMEM_SPEC] * 5,
-        scratch_shapes=[
+        in_specs=[FAR_SPEC] * 7,
+        out_specs=[VMEM_SPEC] * 7,
+        scratch_shapes=[pltpu.VMEM(x.shape, x.dtype) for x in operands]
+        + [
+            pltpu.SemaphoreType.DMA((7,)),
             pltpu.VMEM((2, (rows + 6) * 32, channels // 2), f32),
             pltpu.VMEM((7, rows + 6, cols, channels), f32),
         ],
-        compiler_params=pltpu.CompilerParams(vmem_limit_bytes=32 << 20),
-    )(sums, cells, *halos, kernel, grad_cells)
+        compiler_params=pltpu.CompilerParams(vmem_limit_bytes=58 << 20),
+    )(*operands)
 
 
 def body(
@@ -626,35 +658,29 @@
     down_weight,
     cotangent,
 ):
-    _, rows, cols, channels = field.shape
-    cells = field[0]
-    edges = jnp.concatenate([cells[:, :3], cells[:, cols - 3 :]], axis=1).transpose(1, 0, 2)
-    kernel = depth_kernel.reshape(49, channels)
-    halos = halo(edges, cells, mesh_shape)
-    coarse, grad_cells, grad_depth, grad_edges, packed = block(
-        cells,
-        halos,
-        kernel,
+    channels = field.shape[3]
+    coarse, grad_cells, grad_depth, sums, *grad_halos = main(
+        field[0],
+        depth_kernel,
         layer_norm_gain[None],
         layer_scale[None],
         inner_weight,
         outer_weight,
         down_weight,
         cotangent.reshape(-1, cotangent.shape[3]),
-        place(mesh_shape)[1],
+        mesh_shape,
     )
-    sums, *grad_halos = summed(grad_edges, grad_depth, packed, mesh_shape)
-    grad_inner, grad_outer, grad_down, grad_small, grad_field = finished(
-        sums, grad_depth, grad_halos, kernel, grad_cells
+    grad_inner, grad_outer, grad_down, grad_kernel, grad_gain, grad_scale, grad_field = finished(
+        sums, grad_depth, grad_halos, depth_kernel, grad_cells
     )
     return (
         coarse.reshape(cotangent.shape),
         grad_field.reshape(field.shape),
-        grad_small[:49].reshape(7, 7, channels),
-        grad_small[49],
+        grad_kernel,
+        grad_gain.reshape(channels),
         grad_inner,
         grad_outer,
-        grad_small[50],
+        grad_scale.reshape(channels),
         grad_down,
     )
 

time: 71.5 us -> 63 us (0.88)
  local copies, waits for them, and re-layouts: 10.5 us -> 0.66 us
  Pallas kernels: 59.8 us -> 61.5 us
    unnamed x16 -> x3, local copies, waits for them, and re-layouts: 7.46 us -> 0.66 us
    pallas_call x4 -> x2, Pallas kernels: 59.8 us -> 61.5 us  [the longest x1 53 us: main(): pl.pallas_call(partial(main_body, orders, devices, sizes), name='main', o...]
    slice x3 -> x0, local copies, waits for them, and re-layouts: 1.59 us -> none  [the longest x1 1.02 us: body(): cells[:, :3]]
    reshape x2 -> x0, local copies, waits for them, and re-layouts: 1.46 us -> none  [the longest x1 0.83 us: body(): kernel = depth_kernel.reshape(49, channels)]
where the time goes in v4:
time: 63 us; the launch traced here: 62.8 us
  Pallas kernels  61.5 us (98%)
  between operations  0.67 us (1%)
  local copies, waits for them, and re-layouts  0.66 us (1%)
    pallas_call x1, Pallas kernels, main(): pl.pallas_call(partial(main_body, orders, devices, sizes), name='main', o...  53 us
    pallas_call x1, Pallas kernels, finished(): pl.pallas_call(finish_body, name='finish', out_shape=[jax.ShapeDtypeStruc...  8.51 us

profile of v4, /device:TPU:0, one launch (start us, length us, event | category | flops | bytes accessed | tf_op | source)
XLA Modules:
  0.0 62.8 jit_solution(16915131079503128188)
XLA Ops:
  0.6 53.0 %main.1 = (bf16[128,512]{1,0:T(8,128)(2,1)}, bf16[512,256]{1,0:T(8,128)(2,1)}, bf16[32,16,256]{2,1,0:T(8,128)(2,1)}, bf16[4608,256]{1,0:T(8,128)(2,1)}, bf16[2,3...) custom-call(bf16[32,16,256]{2,1,0:T(8,128)(2,1)} %bitcast.8, ...), custom_call_target="tpu_custom_call" | custom-call | tf_op jit(solution)/shard_map/main/pallas_call | solution.py:384
  53.6 0.0 copy-start
  53.6 8.5 %finish.1 = (f32[256,1024]{1,0:T(8,128)}, f32[1024,256]{1,0:T(8,128)}, f32[1024,512]{1,0:T(8,128)}, f32[7,7,256]{2,1,0:T(8,128)}, f32[1,256]{1,0:T(1,128)}, /*index=5*/f32[1,256]{1,0:T(1,128)}, bf16[512,256]{1,0:T(8,128)(2,1)}) custom-call(bf16[4608,256]{1,0:T(8,128)(2,1)} %get-tuple-element.23.sums_far, bf16[32,16,256]{2,1,0:T(8,128)(2,1)} %get-tuple-element.24.cells_far, ...), custom_call_target="tpu_custom_call" | custom-call | tf_op jit(solution)/shard_map/finish/pallas_call | solution.py:633
  62.2 0.0 copy-done
  62.2 0.7 %copy.17 = bf16[1,16,8,512]{3,2,1,0:T(8,128)(2,1)} copy(bf16[1,16,8,512]{3,2,1,0:T(8,128)(2,1)S(1)} %bitcast.10) | data formatting | bytes 262144
Async XLA Ops:
  53.6 8.5 %copy-start = (bf16[128,512]{1,0:T(8,128)(2,1)S(1)}, bf16[128,512]{1,0:T(8,128)(2,1)}, u32[]{:S(2)}) copy-start(bf16[128,512]{1,0:T(8,128)(2,1)} %get-tuple-element.22) | copy-start | bytes 393220
